TPU v7x, 256 devices: a whole 4x4x8 slice. The times are simulated.
256 devices in a mesh: ctx: 32 (over y, z), head: 8 (over x, core).
Axes of the slice: x: 4, y: 4, z: 8, core: 2. Of those that a mesh axis runs over, the one named last changes fastest.
Arguments:
- queries: bfloat16 [4096, 4096], P('ctx', 'head'), may hold values from -0.75 to 0.75
- keys: bfloat16 [4096, 4096], P('ctx', 'head'), may hold values from -0.75 to 0.75
- values: bfloat16 [4096, 4096], P('ctx', 'head'), may hold values from -0.75 to 0.75
- out_grad: bfloat16 [4096, 4096], P('ctx', 'head'), may hold values from -0.75 to 0.75
- log_decay: float32 [32, 4096], P('head', 'ctx'), may hold values from -1.5 to 0, as said below
- prefix_state: float32 [32, 128, 128], P('head'), may hold values from -3 to 3
- moe_input: bfloat16 [4096, 3072], P('ctx', 'head'), may hold values from -6 to 6
- moe_grad: bfloat16 [4096, 3072], P('ctx', 'head'), may hold values from -6 to 6
- expert_gate: bfloat16 [32, 3072, 4608], P('ctx', None, 'head'), may hold values from -0.109375 to 0.109375
- expert_up: bfloat16 [32, 3072, 4608], P('ctx', None, 'head'), may hold values from -0.109375 to 0.109375
- expert_down: bfloat16 [32, 4608, 3072], P('ctx', 'head'), may hold values from -0.09375 to 0.09375
- expert_ids: int32 [4096, 2], P('ctx'), may hold values from 0 to 31, all different within a row; in each aligned block of 128 rows (0 to 127, 128 to 255, ...) at most 16 rows name the same one
- route_probs: float32 [4096, 2], P('ctx'), may hold values from 0.1 to 1
Outputs:
- query_grad: bfloat16 [4096, 4096], P('ctx', 'head')
- key_grad: bfloat16 [4096, 4096], P('ctx', 'head')
- value_grad: bfloat16 [4096, 4096], P('ctx', 'head')
- moe_input_grad: bfloat16 [4096, 3072], P('ctx', 'head')
Inputs may be any that keep to these rules, and one draw needn't show every extreme that they name: `expert_ids`: each row names two different experts. In each block of 128 rows (one ctx index) no expert is named by more than 16 rows, and in every draw some expert is named by exactly 16 rows of some block. `log_decay`: log of the factor by which a head's state is multiplied at a position.
All inputs are finite; a program needn't handle non-finite values.
Results may differ from a plain program's by a relative error of at most 0.019.
Values may be sent and summed in bfloat16 or wider, within the bound.
A program may use at most 128 MiB of HBM per device.

v0:
```python
import jax
import jax.numpy as jnp
from jax import lax
from jax.sharding import PartitionSpec as P

HIGHEST = lax.Precision.HIGHEST


def carried_in(array, axis, combine, identity, reverse):
    size, mine = (lax.axis_size(axis), lax.axis_index(axis))
    everything = jax.tree.map(
        lambda part, kind: lax.all_gather(part.astype(kind), axis),
        array,
        (jnp.bfloat16, jnp.bfloat16),
    )
    start = jax.tree.map(
        lambda part, zero: jnp.broadcast_to(jnp.asarray(zero, part.dtype), part.shape),
        array,
        identity,
    )

    def lap(k, before):
        at = size - 1 - k if reverse else k
        reached = at > mine if reverse else at < mine
        new = combine(
            before, jax.tree.map(lambda part, own: part[at].astype(own.dtype), everything, array)
        )
        return jax.tree.map(lambda a, b: jnp.where(reached, a, b), new, before)

    return lax.fori_loop(0, size, lap, start)


def decay_factors(log_decay):
    cumulative = jnp.cumsum(log_decay, axis=1)
    totals = cumulative[:, -1]
    token_positions = jnp.arange(log_decay.shape[1], dtype=jnp.int32)
    causal = (token_positions[:, None] >= token_positions[None, :])[None]
    spread = cumulative[:, :, None] - cumulative[:, None, :]
    within = jnp.where(causal, jnp.exp(jnp.where(causal, spread, 0.0)), 0.0)
    tail_decay = jnp.exp(totals[:, None] - cumulative)
    front_decay = jnp.exp(cumulative)
    return (totals, within, tail_decay, front_decay)


def block_summaries(query_heads, key_heads, value_heads, grad_heads, tail_decay, front_decay):
    key_state = jnp.einsum(
        "hsi,hsj->hij", key_heads * tail_decay[:, :, None], value_heads, precision=HIGHEST
    )
    query_state = jnp.einsum(
        "hti,htj->hij", query_heads * front_decay[:, :, None], grad_heads, precision=HIGHEST
    )
    return (key_state, query_state)


def block_grads(
    query_heads,
    key_heads,
    value_heads,
    grad_heads,
    within,
    tail_decay,
    front_decay,
    state_in,
    state_grad,
):
    value_scores = jnp.einsum("hti,hsi->hts", grad_heads, value_heads, precision=HIGHEST) * within
    key_scores = jnp.einsum("hti,hsi->hts", query_heads, key_heads, precision=HIGHEST) * within
    query_out = jnp.einsum("hts,hsi->hti", value_scores, key_heads, precision=HIGHEST)
    query_out = query_out + front_decay[:, :, None] * jnp.einsum(
        "htj,hij->hti", grad_heads, state_in, precision=HIGHEST
    )
    key_out = jnp.einsum("hts,hti->hsi", value_scores, query_heads, precision=HIGHEST)
    key_out = key_out + tail_decay[:, :, None] * jnp.einsum(
        "hsj,hij->hsi", value_heads, state_grad, precision=HIGHEST
    )
    value_out = jnp.einsum("hts,htj->hsj", key_scores, grad_heads, precision=HIGHEST)
    value_out = value_out + tail_decay[:, :, None] * jnp.einsum(
        "hsi,hij->hsj", key_heads, state_grad, precision=HIGHEST
    )
    return (query_out, key_out, value_out)


def chain_combine(earlier, later):
    return (earlier[0] * later[0], later[0][:, None, None] * earlier[1] + later[1])


def swiglu_grads(gate_pre, up_pre, hidden_grad):
    sigmoid = jax.nn.sigmoid(gate_pre)
    gate_grad = hidden_grad * up_pre * sigmoid * (1.0 + gate_pre * (1.0 - sigmoid))
    up_grad = hidden_grad * gate_pre * sigmoid
    return (gate_grad.astype(jnp.bfloat16), up_grad.astype(jnp.bfloat16))


def expert_part(gate_pre, up_pre, hidden_grad, gate_local, up_local):
    gate_grad, up_grad = swiglu_grads(gate_pre, up_pre, hidden_grad)
    partial_value = jnp.einsum(
        "nf,df->nd", gate_grad, gate_local, preferred_element_type=jnp.float32
    )
    partial_value = partial_value + jnp.einsum(
        "nf,df->nd", up_grad, up_local, preferred_element_type=jnp.float32
    )
    rounded = lax.optimization_barrier(partial_value.astype(jnp.bfloat16))
    return rounded.astype(jnp.float32)


def block_slots(block_ids, experts, capacity):
    flat_ids = block_ids.reshape(-1)
    onehot = (flat_ids[:, None] == jnp.arange(experts, dtype=jnp.int32)[None, :]).astype(jnp.int32)
    earlier = jnp.cumsum(onehot, axis=0) - onehot
    slot_rank = jnp.sum(earlier * onehot, axis=1)
    placed = flat_ids * capacity + slot_rank
    pair_index = jnp.arange(flat_ids.shape[0], dtype=jnp.int32)
    source = jnp.zeros((experts * capacity,), jnp.int32).at[placed].set(pair_index // 2)
    filled = jnp.zeros((experts * capacity,), jnp.float32).at[placed].set(1.0)
    return (placed, source, filled)


def shards(
    queries,
    keys,
    values,
    out_grad,
    log_decay,
    prefix_state,
    moe_input,
    moe_grad,
    expert_gate,
    expert_up,
    expert_down,
    expert_ids,
    route_probs,
):
    heads = log_decay.shape[0]
    width = prefix_state.shape[1]
    length = queries.shape[0]

    def to_heads(array):
        return array.astype(jnp.float32).reshape(length, heads, width).transpose(1, 0, 2)

    def from_heads(array):
        return array.transpose(1, 0, 2).reshape(length, heads * width).astype(jnp.bfloat16)

    query_heads = to_heads(queries)
    key_heads = to_heads(keys)
    value_heads = to_heads(values)
    grad_heads = to_heads(out_grad)
    totals, within, tail_decay, front_decay = decay_factors(log_decay)
    key_state, query_state = block_summaries(
        query_heads, key_heads, value_heads, grad_heads, tail_decay, front_decay
    )
    decay_whole = jnp.exp(totals)
    identity_pair = (jnp.ones_like(decay_whole), jnp.zeros_like(key_state))
    before_decay, before_state = carried_in(
        (decay_whole, key_state), "ctx", chain_combine, identity_pair, False
    )
    state_in = before_state + before_decay[:, None, None] * prefix_state
    after_decay, state_grad = carried_in(
        (decay_whole, query_state), "ctx", chain_combine, identity_pair, True
    )
    query_out, key_out, value_out = block_grads(
        query_heads,
        key_heads,
        value_heads,
        grad_heads,
        within,
        tail_decay,
        front_decay,
        state_in,
        state_grad,
    )
    experts = lax.axis_size("ctx")
    capacity = 4 * length // experts
    placed, source, filled = block_slots(expert_ids, experts, capacity)
    gate_local = expert_gate[0]
    up_local = expert_up[0]
    down_local = expert_down[0]

    def buffers(token_rows):
        picked = jnp.take(token_rows, source, axis=0)
        picked = jnp.where(filled[:, None] > 0.0, picked, jnp.zeros_like(picked))
        return picked.reshape(experts, capacity, token_rows.shape[1])

    full_input, full_grad = (
        lax.all_gather(moe_input, "head", axis=1, tiled=True),
        lax.all_gather(moe_grad, "head", axis=1, tiled=True),
    )
    rows_in = lax.all_to_all(buffers(full_input), "ctx", split_axis=0, concat_axis=0, tiled=True)
    rows_grad = lax.all_to_all(buffers(full_grad), "ctx", split_axis=0, concat_axis=0, tiled=True)
    layout = rows_in.shape
    flat_in = rows_in.reshape(-1, layout[2])
    flat_grad = rows_grad.reshape(-1, layout[2])
    gate_pre = jnp.dot(flat_in, gate_local, preferred_element_type=jnp.float32)
    up_pre = jnp.dot(flat_in, up_local, preferred_element_type=jnp.float32)
    hidden_grad = jnp.einsum("nd,fd->nf", flat_grad, down_local, preferred_element_type=jnp.float32)
    partial_value = expert_part(gate_pre, up_pre, hidden_grad, gate_local, up_local).reshape(layout)
    back_rows = lax.psum_scatter(
        partial_value.astype(jnp.bfloat16), "head", scatter_dimension=2, tiled=True
    )
    returned = lax.all_to_all(back_rows, "ctx", split_axis=0, concat_axis=0, tiled=True)
    table = returned.reshape(experts * capacity, -1)
    picked_rows = jnp.take(table, placed, axis=0).astype(jnp.float32).reshape(length, 2, -1)
    moe_input_grad = jnp.sum(picked_rows * route_probs[:, :, None], axis=1).astype(jnp.bfloat16)
    return (from_heads(query_out), from_heads(key_out), from_heads(value_out), moe_input_grad)


def solution(mesh):
    in_specs = (
        P("ctx", "head"),
        P("ctx", "head"),
        P("ctx", "head"),
        P("ctx", "head"),
        P("head", "ctx"),
        P("head", None, None),
        P("ctx", "head"),
        P("ctx", "head"),
        P("ctx", None, "head"),
        P("ctx", None, "head"),
        P("ctx", "head", None),
        P("ctx", None),
        P("ctx", None),
    )
    out_specs = (P("ctx", "head"), P("ctx", "head"), P("ctx", "head"), P("ctx", "head"))
    return jax.shard_map(shards, mesh=mesh, in_specs=in_specs, out_specs=out_specs, check_vma=False)
```

profile of v0, /device:TPU:2, one launch (start us, length us, event | category | flops | bytes accessed | tf_op | source)
XLA Modules:
  0.0 668.2 jit_solution(4718615101521050288)
XLA Ops:
  13.4 1.9 reduce-window.6
  20.5 14.9 %all_gather.29 = bf16[128,3072]{1,0:T(8,128)(2,1)} all-gather(bf16[128,384]{1,0:T(8,128)(2,1)} %param.26), channel_id=1, replica_groups=mesh['ctx'=32,'head'=8] {'head'}, dimensions={1}, use_global_device_ids=true | all-gather | bytes 884736 | tf_op jit(solution)/shard_map/all_gather | solution.py:185
  35.4 14.8 %all_gather.30 = bf16[128,3072]{1,0:T(8,128)(2,1)} all-gather(bf16[128,384]{1,0:T(8,128)(2,1)} %param.25), channel_id=1, replica_groups=mesh['ctx'=32,'head'=8] {'head'}, dimensions={1}, use_global_device_ids=true | all-gather | bytes 884736 | tf_op jit(solution)/shard_map/all_gather | solution.py:184
  50.2 8.3 %gather_fusion.1 = bf16[512,3072]{1,0:T(8,128)(2,1)} fusion(bf16[128,3072]{1,0:T(8,128)(2,1)} %all_gather.29, s32[1024]{0:T(1024)S(1)} %pad_clamp_fusion.1), kind=kCustom, calls=%fused_computation.clone | custom fusion | bytes 6293504 | tf_op jit(solution)/shard_map/jit(_take)/gather | solution.py:179
  58.5 8.3 %gather_fusion.2 = bf16[512,3072]{1,0:T(8,128)(2,1)} fusion(bf16[128,3072]{1,0:T(8,128)(2,1)} %all_gather.30, s32[1024]{0:T(1024)S(1)} %pad_clamp_fusion.1), kind=kCustom, calls=%fused_computation.1.clone | custom fusion | bytes 6293504 | tf_op jit(solution)/shard_map/jit(_take)/gather | solution.py:179
  68.9 5.0 select_select_fusion
  73.9 11.7 %all-to-all-start.1 = ((bf16[32,16,3072]{2,1,0:T(8,128)(2,1)}), bf16[32,16,3072]{2,1,0:T(8,128)(2,1)}, u32[]{:S(2)}, u32[]{:S(2)}) async-start(bf16[32,16,3072]{2,1,0:T(8,128)(2,1)} %bitcast.205), calls=%async_computation.1 | async-start | bytes 6291456 | tf_op jit(solution)/shard_map/all_to_all | solution.py:187
  85.9 74.8 %all-to-all-done.1 = bf16[32,16,3072]{2,1,0:T(8,128)(2,1)} async-done(((bf16[32,16,3072]{2,1,0:T(8,128)(2,1)}), bf16[32,16,3072]{2,1,0:T(8,128)(2,1)}, u32[]{:S(2)}, u32[]{:S(2)}) %all-to-all-start.1) | async-done | bytes 3145760 | tf_op jit(solution)/shard_map/all_to_all | solution.py:187
  160.7 4.8 all-to-all-start
  166.9 2.1 convolution_convert_fusion.1
  169.3 6.0 fusion.4
  175.3 72.2 %all-to-all-done = bf16[32,16,3072]{2,1,0:T(8,128)(2,1)} async-done(((bf16[32,16,3072]{2,1,0:T(8,128)(2,1)}), bf16[32,16,3072]{2,1,0:T(8,128)(2,1)}, u32[]{:S(2)}, u32[]{:S(2)}) %all-to-all-start) | async-done | bytes 3145760 | tf_op jit(solution)/shard_map/all_to_all | solution.py:188
  247.5 6.1 fusion.9
  253.6 11.1 %fusion.2 = f32[512,3072]{1,0:T(8,128)} fusion(bf16[1,3072,576]{1,2,0:T(8,128)(2,1)} %param.27, f32[512,576]{0,1:T(8,128)} %fusion.9, bf16[512,3072]{1,0:T(8,128)(2,1)} %bitcast.31, bf16[1,3072,576]{1,2,0:T(8,128)(2,1)S(1)} %copy-done, f32[512,576]{0,1:T(8,128)} %fusion.4), kind=kOutput, calls=%fused_computation.14 | convolution fusion | flops 3626827776 | bytes 18874368 | tf_op jit(solution)/shard_map/nf,df->nd/dot_general | solution.py:96
  264.7 6.8 %add_convert_fusion = bf16[512,3072]{1,0:T(8,128)(2,1)} fusion(f32[512,3072]{1,0:T(8,128)} %fusion.2, bf16[1,3072,576]{1,2,0:T(8,128)(2,1)S(1)} %copy-done, f32[512,576]{0,1:T(8,128)} %fusion.9, f32[512,576]{0,1:T(8,128)} %fusion.4), kind=kOutput, calls=%fused_computation.13 | convolution fusion | flops 1816854528 | bytes 15335424 | tf_op jit(solution)/shard_map/nf,df->nd/dot_general | solution.py:99
  271.5 21.7 %copy.105 = bf16[32,16,3072]{1,0,2:T(8,128)(2,1)} copy(bf16[32,16,3072]{2,1,0:T(8,128)(2,1)} %bitcast.206) | data formatting | bytes 6291456
  293.1 42.0 %reshape.267 = bf16[3072,512]{1,0:T(8,128)(2,1)} reshape(bf16[3072,32,16]{2,1,0:T(8,128)(2,1)} %bitcast.202) | data formatting | bytes 6291456
  337.1 2.1 convolution_convert_fusion
  343.9 2.0 convolution_bitcast_fusion.5
  345.9 1.9 convolution_bitcast_fusion.3
  347.8 1.9 convolution_multiply_fusion
  357.0 73.9 %all-reduce = bf16[128]{0:T(256)(128)(2,1)} all-reduce(bf16[128]{0:T(256)(128)(2,1)} %dynamic-update-slice), channel_id=2, replica_groups=mesh['ctx'=32,'head'=8] {'ctx'}, use_global_device_ids=true, to_apply=%add | all-reduce | flops 128 | bytes 512
  432.3 2.0 convolution_bitcast_fusion.1
  434.3 96.2 %while.32 = (s32[]{:T(128)}, f32[4]{0:T(128)}, f32[4,128,128]{2,1,0:T(8,128)}, s32[]{:T(128)}, bf16[32,4]{1,0:T(8,128)(2,1)}, /*index=5*/bf16[32,4,128,128]{3,2,1,0:T(8,128)(2,1)}, s32[]{:T(128)}, s32[]{:T(128)}) while((s32[]{:T(128)}, f32[4]{0:T(128)}, f32[4,128,128]{2,1,0:T(8,128)}, s32[]{:T(128)}, bf16[32,4]{1,0:T(8,128)(2,1)}, ...), condition=%wide.region_2.3_spmd.clone, body=%wide.region_1.2_spmd.clone.sunk | while | flops 327700 | bytes 655547 | solution.py:30
  530.6 4.6 reshape.268
  535.2 5.1 copy.106
  540.3 4.6 all-to-all-start.2
  544.9 97.5 %while.33 = (s32[]{:T(128)}, f32[4,128,128]{2,1,0:T(8,128)}, s32[]{:T(128)}, bf16[32,4]{1,0:T(8,128)(2,1)}, bf16[32,4,128,128]{3,2,1,0:T(8,128)(2,1)}, /*index=5*/s32[]{:T(128)}, s32[]{:T(128)}, s32[]{:T(128)}, s32[]{:T(128)}) while((s32[]{:T(128)}, f32[4,128,128]{2,1,0:T(8,128)}, s32[]{:T(128)}, bf16[32,4]{1,0:T(8,128)(2,1)}, ...), condition=%wide.region_4.5_spmd.clone, body=%wide.region_3.4_spmd.clone.sunk | while | flops 327692 | bytes 655567 | solution.py:30
  549.1 1.9 fusion.91
  552.1 1.9 fusion.91
  555.2 1.9 fusion.91
  558.2 1.9 fusion.91
  561.3 1.9 fusion.91
  564.3 1.9 fusion.91
  567.4 1.9 fusion.91
  570.4 1.9 fusion.91
  573.5 1.9 fusion.91
  576.5 1.9 fusion.91
  622.2 1.9 fusion.91
  625.3 1.9 fusion.91
  628.3 1.9 fusion.91
  631.4 1.9 fusion.91
  634.4 1.9 fusion.91
  642.4 2.2 fusion.29
  646.2 2.1 fusion.30
  650.0 2.1 fusion.31
  653.8 3.0 gather_fusion
  658.5 2.3 multiply_reduce_fusion
  (177 shorter events, 201.7 us)
Async XLA Ops:
  8.0 245.6 %copy-start = (bf16[1,3072,576]{1,2,0:T(8,128)(2,1)S(1)}, bf16[1,3072,576]{1,2,0:T(8,128)(2,1)}, u32[]{:S(2)}) copy-start(bf16[1,3072,576]{1,2,0:T(8,128)(2,1)} %param.28) | copy-start | bytes 10616836
  18.9 48.4 %copy-start.3 = (s32[256,1]{0,1:T(1,128)}, s32[256,1]{0,1:T(1,128)S(1)}, u32[]{:S(2)}) copy-start(s32[256,1]{0,1:T(1,128)S(1)} %compare_select_fusion) | copy-start | bytes 3076
  73.9 11.7 %copy-start.4 = (f32[4,128]{1,0:T(4,128)S(1)}, f32[4,128]{1,0:T(4,128)}, u32[]{:S(2)}) copy-start(f32[4,128]{1,0:T(4,128)} %param.23) | copy-start | bytes 6148
  73.9 86.8 %all-to-all-start.1 = ((bf16[32,16,3072]{2,1,0:T(8,128)(2,1)}), bf16[32,16,3072]{2,1,0:T(8,128)(2,1)}, u32[]{:S(2)}, u32[]{:S(2)}) async-start(bf16[32,16,3072]{2,1,0:T(8,128)(2,1)} %bitcast.205), calls=%async_computation.1 | async-start | bytes 6291456 | tf_op jit(solution)/shard_map/all_to_all | solution.py:187
  160.7 86.7 %all-to-all-start = ((bf16[32,16,3072]{2,1,0:T(8,128)(2,1)}), bf16[32,16,3072]{2,1,0:T(8,128)(2,1)}, u32[]{:S(2)}, u32[]{:S(2)}) async-start(bf16[32,16,3072]{2,1,0:T(8,128)(2,1)} %bitcast.204), calls=%async_computation | async-start | bytes 6291456 | tf_op jit(solution)/shard_map/all_to_all | solution.py:188
  165.6 268.8 %all-gather.6.cloned.1.call-start = ((), (), s32[]{:S(2)}) async-start(), calls=%async_computation.4 | async-start | bytes 4325376 | tf_op jit(solution)/shard_map/all_gather | solution.py:12
  166.3 0.6 copy-start.1
  169.0 361.5 %reduce-scatter.4.cloned.1.call-start = ((), (), s32[]{:S(2)}) async-start(), calls=%async_computation.6 | async-start | bytes 3538944
  335.1 15.5 %copy-start.2 = (s32[128,2]{0,1:T(2,128)S(1)}, s32[128,2]{0,1:T(2,128)}, u32[]{:S(2)}) copy-start(s32[128,2]{0,1:T(2,128)} %param.30) | copy-start | bytes 3076
  335.2 209.8 %all-gather.8.cloned.1.call-start = ((), (), s32[]{:S(2)}) async-start(), calls=%async_computation.5 | async-start | bytes 4325376 | tf_op jit(solution)/shard_map/all_gather | solution.py:12
  540.3 113.5 %all-to-all-start.2 = ((bf16[32,16,384]{2,1,0:T(8,128)(2,1)}), bf16[32,16,384]{2,1,0:T(8,128)(2,1)}, u32[]{:S(2)}, u32[]{:S(2)}) async-start(bf16[32,16,384]{2,1,0:T(8,128)(2,1)} %copy.106), calls=%async_computation.2 | async-start | bytes 786432 | tf_op jit(solution)/shard_map/all_to_all | solution.py:199
Sparse Core Ops, SparseCore 0:
  169.6 97.4 all-gather.5
  339.3 78.6 all-gather.7
Sparse Core Ops, SparseCore 1:
  335.2 31.5 reduce-scatter.3
where the time goes:
time: 674 us; the launch traced here: 668 us
  other arithmetic  210 us (31%)
  waiting for transfers between devices  147 us (22%)
  local copies, waits for them, and re-layouts  120 us (18%)
  blocking collectives  104 us (15%)
  matrix products  49.8 us (7%)
  starting transfers between devices  21.7 us (3%)
  between operations  16.3 us (2%)
    select_n x96, other arithmetic, lap(): return jax.tree.map(lambda a, b: jnp.where(reached, a, b), new, before)  155 us
    unnamed x22, local copies, waits for them, and re-layouts  84.9 us
    all_to_all x1, waiting for transfers between devices, shards(): lax.all_to_all(buffers(full_input), 'ctx', split_axis=0, concat_axis=0, t...  74.8 us
    unnamed x1, blocking collectives  73.9 us
    all_to_all x1, waiting for transfers between devices, shards(): lax.all_to_all(buffers(full_grad), 'ctx', split_axis=0, concat_axis=0, ti...  72.2 us
    convert_element_type x32, other arithmetic, lap(): part[at].astype(own.dtype)  38.3 us
    gather x2, local copies, waits for them, and re-layouts, buffers(): picked = jnp.take(token_rows, source, axis=0)  16.6 us
    all_gather x1, blocking collectives, shards(): lax.all_gather(moe_grad, 'head', axis=1, tiled=True)  14.9 us
  transfers between devices with their start and end apart: 6, of which 2 were waited for; matrix products, arithmetic and copies ran while one was open for 50% of the time, Pallas kernels for 0%

commit v1 on v0

v1 whole, which is shorter than its diff:
```python
import functools

import jax
import jax.numpy as jnp
from jax import lax
from jax.experimental import pallas as pl
from jax.experimental.pallas import tpu as pltpu
from jax.sharding import PartitionSpec as P

F32 = jnp.float32
BF16 = jnp.bfloat16
MESH = pl.DeviceIdType.MESH
NX = 4
LANES = 128


def dot(a, b):
    return jnp.dot(a, b, preferred_element_type=F32)


def dot_t(a, b):
    return lax.dot_general(a, b, (((1,), (1,)), ((), ())), preferred_element_type=F32)


def dot_l(a, b):
    return lax.dot_general(a, b, (((0,), (0,)), ((), ())), preferred_element_type=F32)


def pieces(value, count):
    parts = []
    for _ in range(count):
        part = value.astype(BF16)
        parts.append(part)
        value = value - part.astype(F32)
    return parts


def kernel(
    size,
    q_ref, k_ref, v_ref, g_ref, decay_ref, prefix_ref, in_ref, grad_ref, gate_hbm, up_hbm, down_hbm, ids_ref, probs_ref,
    dq_ref, dk_ref, dv_ref, dx_ref,
    gate, up, down, out_rows, rows, acc_gate, acc_up, acc_hidden, part, part_in, total, far_left, far_right, near_left,
    near_right, back, table, weights, state_out, state_all, scan_out, state, local, front_s, tail_s,
    w_sem, one_sem, a2a_recv, ring_recv, sib_recv, send_sem, part_recv, far_recv, near_recv, back_recv,
):
    E, NY, NZ, T, CAP, DC, HL, NG = size
    EG = E // NG
    NR = EG * CAP
    HALF = NR // 2
    W = 2 * DC
    SR = HL * LANES // E
    SHIFT = NZ.bit_length() - 1

    c, h = lax.axis_index("ctx"), lax.axis_index("head")
    x, core = h // 2, h % 2
    y, z = c // NZ, c % NZ
    x_left, x_right, x_far = (x + NX - 1) % NX, (x + 1) % NX, (x + 2) % NX
    right = (c, x_right * 2 + core)
    left = (c, x_left * 2 + core)
    sibling = (c, x * 2 + 1 - core)
    mine = pl.ds(pl.multiple_of(core * DC, LANES), DC)
    other = pl.ds(pl.multiple_of((1 - core) * DC, LANES), DC)

    def forth(d):
        return ((y + d // NZ) % NY) * NZ + (z + d % NZ) % NZ

    def back_to(d):
        return ((y + NY - d // NZ) % NY) * NZ + (z + NZ - d % NZ) % NZ

    def group(g):
        return pl.ds(g * NR, NR)

    def remote(src, dst, send, recv, device):
        return pltpu.make_async_remote_copy(
            src_ref=src, dst_ref=dst, send_sem=send, recv_sem=recv, device_id=device, device_id_type=MESH
        )

    def arrived(ref, recv):
        remote(ref, ref, recv, recv, right).wait_recv()

    def sent(ref, send):
        remote(ref, ref, send, send, right).wait_send()

    barrier = pltpu.get_barrier_semaphore()

    def greet(d, carry):
        pl.semaphore_signal(barrier, inc=1, device_id=(forth(d), h), device_id_type=MESH)
        return carry

    lax.fori_loop(1, E, greet, 0)
    for device in (right, left, sibling):
        pl.semaphore_signal(barrier, inc=1, device_id=device, device_id_type=MESH)

    loads = [
        pltpu.make_async_copy(hbm.at[0], vmem, w_sem.at[i])
        for i, (hbm, vmem) in enumerate(((gate_hbm, gate), (up_hbm, up), (down_hbm, down)))
    ]
    for load in loads:
        load.start()

    lane = lax.broadcasted_iota(jnp.int32, (T, E), 1)
    expert = (((y + (lane >> SHIFT)) & (NY - 1)) << SHIFT) + ((z + (lane & (NZ - 1))) & (NZ - 1))
    first = (ids_ref[:, 0:1] == expert).astype(F32)
    second = (ids_ref[:, 1:2] == expert).astype(F32)
    named = first + second
    t_row = lax.broadcasted_iota(jnp.int32, (T, T), 0)
    t_col = lax.broadcasted_iota(jnp.int32, (T, T), 1)
    earlier = dot((t_row > t_col).astype(F32).astype(BF16), named.astype(BF16))
    slot = jnp.where(named > 0.5, earlier, -1.0).astype(BF16)
    r_row = lax.broadcasted_iota(jnp.int32, (E * CAP, E), 0)
    e_col = lax.broadcasted_iota(jnp.int32, (E * CAP, E), 1)
    spread = (r_row // CAP == e_col).astype(F32).astype(BF16)
    want = (lax.broadcasted_iota(jnp.int32, (E * CAP, T), 0) % CAP).astype(F32)
    pick = (dot_t(spread, slot) == want).astype(F32).astype(BF16)
    out_rows[:, 0] = dot(pick, in_ref[...]).astype(BF16).reshape(E, CAP, DC)
    out_rows[:, 1] = dot(pick, grad_ref[...]).astype(BF16).reshape(E, CAP, DC)

    pl.semaphore_wait(barrier, E - 1 + 3)

    def dispatch(d, carry):
        remote(
            out_rows.at[d], rows.at[:, x, pl.ds(d * CAP, CAP), mine], send_sem.at[0], a2a_recv.at[d // EG], (forth(d), h)
        ).start()
        return carry

    own = pltpu.make_async_copy(out_rows.at[0], rows.at[:, x, pl.ds(0, CAP), mine], one_sem.at[0])
    own.start()
    lax.fori_loop(1, E, dispatch, 0)

    cum = jnp.zeros((HL, T), F32)
    upto = (t_row <= t_col).astype(F32).astype(BF16)
    for piece in pieces(decay_ref[...], 3):
        cum = cum + dot(piece, upto)
    slab = lax.broadcasted_iota(jnp.int32, (LANES, LANES), 0) % SR
    for i in range(HL):
        cols = slice(i * LANES, (i + 1) * LANES)
        along = jnp.broadcast_to(cum[i : i + 1, :], (T, T))
        down_t = along.T
        total_b = jnp.broadcast_to(down_t[T - 1 : T, :], (T, T))
        front_s[i] = jnp.exp(down_t)
        tail_s[i] = jnp.exp(total_b - down_t)
        q, k, v, g = q_ref[:, cols], k_ref[:, cols], v_ref[:, cols], g_ref[:, cols]
        state_out[cols, 0:LANES] = dot_l((k.astype(F32) * tail_s[i]).astype(BF16), v).astype(BF16)
        state_out[cols, LANES : 2 * LANES] = dot_l((q.astype(F32) * front_s[i]).astype(BF16), g).astype(BF16)
        d0, d1, d2 = [piece.astype(F32) for piece in pieces(jnp.exp(total_b), 3)]
        state_out[cols, 2 * LANES :] = jnp.where(slab == 0, d0, jnp.where(slab == 1, d1, d2)).astype(BF16)

    def slices(ref, p):
        return ref.at[pl.ds(pl.multiple_of(p * SR, SR), SR), :]

    def states(d, carry):
        remote(slices(state_out, forth(d)), slices(state_all, c), send_sem.at[1], one_sem.at[1], (forth(d), h)).start()
        return carry

    own_state = pltpu.make_async_copy(slices(state_out, c), slices(state_all, c), one_sem.at[2])
    own_state.start()
    lax.fori_loop(1, E, states, 0)

    for i in range(HL):
        cols = slice(i * LANES, (i + 1) * LANES)
        along = jnp.broadcast_to(cum[i : i + 1, :], (T, T))
        down_t = along.T
        q, k, v, g = q_ref[:, cols], k_ref[:, cols], v_ref[:, cols], g_ref[:, cols]
        low, high = t_row >= t_col, t_row <= t_col
        within = jnp.where(low, jnp.exp(jnp.where(low, down_t - along, 0.0)), 0.0)
        within_t = jnp.where(high, jnp.exp(jnp.where(high, along - down_t, 0.0)), 0.0)
        local[0, :, cols] = dot((dot_t(g, v) * within).astype(BF16), k)
        local[1, :, cols] = dot((dot_t(v, g) * within_t).astype(BF16), q)
        local[2, :, cols] = dot((dot_t(k, q) * within_t).astype(BF16), g)

    chance = first * probs_ref[:, 0:1] + second * probs_ref[:, 1:2]
    pick_t = dot_t(slot, spread) == (lax.broadcasted_iota(jnp.int32, (T, E * CAP), 1) % CAP).astype(F32)
    for i, piece in enumerate(pieces(chance, 3)):
        weights[i] = jnp.where(pick_t, dot_t(piece, spread), 0.0).astype(BF16)

    def scan_states():
        own_state.wait()
        arrived(state_all.at[pl.ds(0, (E - 1) * SR), :], one_sem.at[1])

        def step(reverse, column, i, carried):
            at = E - 1 - i if reverse else i
            tile = slices(state_all, at)[...].astype(F32)
            factor = tile[0:1, 2 * LANES :] + tile[1:2, 2 * LANES :] + tile[2:3, 2 * LANES :]
            columns = slice(column * LANES, (column + 1) * LANES)
            slices(scan_out, at)[:, columns] = carried.astype(BF16)
            return factor * carried + tile[:, columns]

        lax.fori_loop(0, E, functools.partial(step, False, 0), slices(prefix_ref, c)[...])
        lax.fori_loop(0, E, functools.partial(step, True, 1), jnp.zeros((SR, LANES), F32))

        def give(d, carry):
            remote(slices(scan_out, forth(d)), slices(state, c), send_sem.at[2], one_sem.at[3], (forth(d), h)).start()
            return carry

        own_scan.start()
        lax.fori_loop(1, E, give, 0)

    own_scan = pltpu.make_async_copy(slices(scan_out, c), slices(state, c), one_sem.at[4])

    def finish_states():
        own_scan.wait()
        arrived(state.at[pl.ds(0, (E - 1) * SR), :], one_sem.at[3])
        for i in range(HL):
            cols = slice(i * LANES, (i + 1) * LANES)
            k, v, g = k_ref[:, cols], v_ref[:, cols], g_ref[:, cols]
            s_in, s_grad = state[cols, 0:LANES], state[cols, LANES : 2 * LANES]
            dq_ref[:, cols] = (local[0, :, cols] + front_s[i] * dot_t(g, s_in)).astype(BF16)
            dk_ref[:, cols] = (local[1, :, cols] + tail_s[i] * dot_t(v, s_grad)).astype(BF16)
            dv_ref[:, cols] = (local[2, :, cols] + tail_s[i] * dot(k, s_grad)).astype(BF16)

    def to_sibling(ref, which, send):
        remote(ref, ref, send_sem.at[send], sib_recv.at[which], sibling).start()

    def gather_1(g):
        if g == 0:
            own.wait()
        lead = CAP if g == 0 else 0
        arrived(rows.at[:, x, pl.ds(g * NR + lead, NR - lead), mine], a2a_recv.at[g])
        ref = rows.at[:, x, group(g), mine]
        remote(ref, ref, send_sem.at[3], ring_recv.at[g, 0], right).start()
        remote(ref, ref, send_sem.at[4], ring_recv.at[g, 1], left).start()
        to_sibling(ref, (g, 0), 7)

    def gather_2(g):
        from_left, from_right = rows.at[:, x_left, group(g), mine], rows.at[:, x_right, group(g), mine]
        arrived(from_left, ring_recv.at[g, 0])
        ref = rows.at[0, x_left, group(g), mine]
        remote(ref, ref, send_sem.at[5], ring_recv.at[g, 2], right).start()
        to_sibling(from_left, (g, 1), 8)
        arrived(from_right, ring_recv.at[g, 1])
        ref = rows.at[1, x_right, group(g), mine]
        remote(ref, ref, send_sem.at[6], ring_recv.at[g, 3], left).start()
        to_sibling(from_right, (g, 2), 9)

    def gather_3(g):
        for i in range(2):
            ref = rows.at[i, x_far, group(g), mine]
            arrived(ref, ring_recv.at[g, 2 + i])
            to_sibling(ref, (g, 3 + i), 10 + i)

    def expert(g):
        for i, at in enumerate((x, x_left, x_right, x_far)):
            if i < 3:
                arrived(rows.at[:, at, group(g), other], sib_recv.at[g, i])
            else:
                arrived(rows.at[0, at, group(g), other], sib_recv.at[g, 3])
                arrived(rows.at[1, at, group(g), other], sib_recv.at[g, 4])
            deep = pl.ds(pl.multiple_of(at * W, LANES), W)
            r_in, r_grad = rows[0, at, group(g), :], rows[1, at, group(g), :]
            for acc, value in (
                (acc_gate, dot(r_in, gate[deep, :])),
                (acc_up, dot(r_in, up[deep, :])),
                (acc_hidden, dot_t(r_grad, down[:, deep])),
            ):
                acc[...] = value if i == 0 else acc[...] + value
        gate_pre, up_pre, hidden = acc_gate[...], acc_up[...], acc_hidden[...]
        sig = 1.0 / (1.0 + jnp.exp(-gate_pre))
        gate_grad = (hidden * up_pre * sig * (1.0 + gate_pre * (1.0 - sig))).astype(BF16)
        up_grad = (hidden * gate_pre * sig).astype(BF16)

        def column(i, carry):
            deep = pl.ds(pl.multiple_of(i * W, LANES), W)
            part[i, group(g), :] = (dot_t(gate_grad, gate[deep, :]) + dot_t(up_grad, up[deep, :])).astype(BF16)
            return carry

        lax.fori_loop(0, NX, column, 0)

    def reduce_1(g):
        remote(
            part.at[:, group(g), other], part_in.at[:, group(g), :], send_sem.at[12], part_recv.at[g], sibling
        ).start()

    def pair_sum(at, span):
        return part[at, span, mine].astype(F32) + part_in[at, span, :].astype(F32)

    def reduce_2(g):
        arrived(part_in.at[:, group(g), :], part_recv.at[g])
        total[0, group(g), :] = pair_sum(x_far, group(g)).astype(BF16)
        remote(
            total.at[0, pl.ds(g * NR, HALF), :], far_left.at[pl.ds(g * HALF, HALF), :], send_sem.at[13], far_recv.at[g, 0], right
        ).start()
        remote(
            total.at[0, pl.ds(g * NR + HALF, HALF), :], far_right.at[pl.ds(g * HALF, HALF), :], send_sem.at[14], far_recv.at[g, 1], left
        ).start()

    def reduce_3(g):
        half = pl.ds(g * HALF, HALF)
        lower, upper = pl.ds(g * NR, HALF), pl.ds(g * NR + HALF, HALF)
        arrived(far_left.at[half, :], far_recv.at[g, 0])
        total[1, lower, :] = (pair_sum(x_right, lower) + far_left[half, :].astype(F32)).astype(BF16)
        total[1, upper, :] = pair_sum(x_right, upper).astype(BF16)
        remote(
            total.at[1, group(g), :], near_left.at[group(g), :], send_sem.at[15], near_recv.at[g, 0], right
        ).start()
        arrived(far_right.at[half, :], far_recv.at[g, 1])
        total[2, lower, :] = pair_sum(x_left, lower).astype(BF16)
        total[2, upper, :] = (pair_sum(x_left, upper) + far_right[half, :].astype(F32)).astype(BF16)
        remote(
            total.at[2, group(g), :], near_right.at[group(g), :], send_sem.at[16], near_recv.at[g, 1], left
        ).start()

    def slots(ref, d):
        return ref.at[pl.ds(pl.multiple_of(d * CAP, CAP), CAP), :]

    own_back = pltpu.make_async_copy(slots(back, 0), slots(table, 0), one_sem.at[5])

    def reduce_4(g):
        arrived(near_left.at[group(g), :], near_recv.at[g, 0])
        arrived(near_right.at[group(g), :], near_recv.at[g, 1])
        value = near_left[group(g), :].astype(F32) + near_right[group(g), :].astype(F32)
        back[group(g), :] = (pair_sum(x, group(g)) + value).astype(BF16)

        def give(d, carry):
            remote(slots(back, d), slots(table, d), send_sem.at[17], back_recv.at[0], (back_to(d), h)).start()
            return carry

        if g == 0:
            own_back.start()
        lax.fori_loop(max(g * EG, 1), (g + 1) * EG, give, 0)

    for load in loads:
        load.wait()
    for i in range(NG + 5):
        for ahead, stage in enumerate((gather_1, gather_2, gather_3)):
            if 0 <= i - ahead < NG:
                stage(i - ahead)
        if i == NG - 1:
            scan_states()
        if 0 <= i - 2 < NG:
            expert(i - 2)
            reduce_1(i - 2)
        if i == NG + 1:
            finish_states()
        for ahead, stage in ((3, reduce_2), (4, reduce_3), (5, reduce_4)):
            if 0 <= i - ahead < NG:
                stage(i - ahead)

    own_back.wait()
    arrived(table.at[pl.ds(0, (E - 1) * CAP), :], back_recv.at[0])
    found = table[...]
    dx_ref[...] = (dot(weights[0], found) + dot(weights[1], found) + dot(weights[2], found)).astype(BF16)

    ring, half_ring = rows.at[:, 0, :, 0:DC], rows.at[0, 0, :, 0:DC]
    for i, ref in (
        (0, out_rows.at[pl.ds(1, E - 1)]),
        (1, state_out.at[pl.ds(0, (E - 1) * SR), :]),
        (2, scan_out.at[pl.ds(0, (E - 1) * SR), :]),
        (3, ring), (4, ring), (5, half_ring), (6, half_ring),
        (7, ring), (8, ring), (9, ring), (10, half_ring), (11, half_ring),
        (12, part_in), (13, far_left), (14, far_right), (15, near_left), (16, near_right),
        (17, back.at[pl.ds(0, (E - 1) * CAP), :]),
    ):
        sent(ref, send_sem.at[i])


def solution(mesh):
    E = mesh.shape["ctx"]
    NZ = min(8, E // 2)

    def shards(queries, keys, values, out_grad, log_decay, prefix_state, moe_input, moe_grad, gate, up, down, ids, probs):
        T, HL = queries.shape[0], log_decay.shape[0]
        DC, D, FL = moe_input.shape[1], gate.shape[1], gate.shape[2]
        CAP = 4 * T // E
        NG = min(4, E // 2)
        ROWS, NR = E * CAP, E * CAP // NG
        vmem = pl.BlockSpec(memory_space=pltpu.VMEM)
        hbm = pl.BlockSpec(memory_space=pl.ANY)
        size = (E, E // NZ, NZ, T, CAP, DC, HL, NG)
        dma = pltpu.SemaphoreType.DMA
        return pl.pallas_call(
            functools.partial(kernel, size),
            out_shape=[jax.ShapeDtypeStruct((T, HL * LANES), BF16)] * 3 + [jax.ShapeDtypeStruct((T, DC), BF16)],
            in_specs=[vmem] * 8 + [hbm] * 3 + [vmem] * 2,
            out_specs=[vmem] * 4,
            scratch_shapes=[
                pltpu.VMEM((D, FL), BF16),
                pltpu.VMEM((D, FL), BF16),
                pltpu.VMEM((FL, D), BF16),
                pltpu.VMEM((E, 2, CAP, DC), BF16),
                pltpu.VMEM((2, NX, ROWS, 2 * DC), BF16),
                pltpu.VMEM((NR, FL), F32),
                pltpu.VMEM((NR, FL), F32),
                pltpu.VMEM((NR, FL), F32),
                pltpu.VMEM((NX, ROWS, 2 * DC), BF16),
                pltpu.VMEM((NX, ROWS, DC), BF16),
                pltpu.VMEM((3, ROWS, DC), BF16),
                pltpu.VMEM((ROWS // 2, DC), BF16),
                pltpu.VMEM((ROWS // 2, DC), BF16),
                pltpu.VMEM((ROWS, DC), BF16),
                pltpu.VMEM((ROWS, DC), BF16),
                pltpu.VMEM((ROWS, DC), BF16),
                pltpu.VMEM((ROWS, DC), BF16),
                pltpu.VMEM((3, T, ROWS), BF16),
                pltpu.VMEM((HL * LANES, 3 * LANES), BF16),
                pltpu.VMEM((HL * LANES, 3 * LANES), BF16),
                pltpu.VMEM((HL * LANES, 2 * LANES), BF16),
                pltpu.VMEM((HL * LANES, 2 * LANES), BF16),
                pltpu.VMEM((3, T, HL * LANES), F32),
                pltpu.VMEM((HL, T, LANES), F32),
                pltpu.VMEM((HL, T, LANES), F32),
                dma((3,)),
                dma((6,)),
                dma((NG,)),
                dma((NG, 4)),
                dma((NG, 5)),
                dma((18,)),
                dma((NG,)),
                dma((NG, 2)),
                dma((NG, 2)),
                dma((1,)),
            ],
            compiler_params=pltpu.CompilerParams(
                collective_id=0, has_side_effects=True, vmem_limit_bytes=52 * 1024 * 1024
            ),
        )(
            queries, keys, values, out_grad, log_decay, prefix_state.reshape(HL * LANES, LANES),
            moe_input, moe_grad, gate, up, down, ids, probs,
        )

    in_specs = (
        P("ctx", "head"),
        P("ctx", "head"),
        P("ctx", "head"),
        P("ctx", "head"),
        P("head", "ctx"),
        P("head", None, None),
        P("ctx", "head"),
        P("ctx", "head"),
        P("ctx", None, "head"),
        P("ctx", None, "head"),
        P("ctx", "head", None),
        P("ctx", None),
        P("ctx", None),
    )
    out_specs = (P("ctx", "head"), P("ctx", "head"), P("ctx", "head"), P("ctx", "head"))
    return jax.shard_map(shards, mesh=mesh, in_specs=in_specs, out_specs=out_specs, check_vma=False)
```

time: 674 us -> 97.9 us (0.15)
  other arithmetic: 210 us -> 0 us
  waiting for transfers between devices: 147 us -> 0 us
  blocking collectives: 104 us -> 0 us
  local copies, waits for them, and re-layouts: 120 us -> 16.5 us
  Pallas kernels: 0 us -> 80.3 us
  matrix products: 49.8 us -> 0 us
  starting transfers between devices: 21.7 us -> 0 us
  between operations: 16.3 us -> 0.73 us
    select_n x100 -> x0, other arithmetic: 161 us -> none  [the longest x96 155 us: lap(): return jax.tree.map(lambda a, b: jnp.where(reached, a, b), new, before)]
    all_to_all x3 -> x0, waiting for transfers between devices: 147 us -> none  [the longest x1 74.8 us: shards(): lax.all_to_all(buffers(full_input), 'ctx', split_axis=0, concat_axis=0, t...]
    pallas_call x0 -> x1, Pallas kernels: none -> 80.3 us  [shards(): pl.pallas_call(functools.partial(kernel, size), out_shape=[jax.ShapeDtype...]
    unnamed x1 -> x0, blocking collectives: 73.9 us -> none
    unnamed x22 -> x24, local copies, waits for them, and re-layouts: 84.9 us -> 16.5 us
    dot_general x14 -> x0, matrix products: 49.8 us -> none  [the longest x1 11.1 us: expert_part(): jnp.einsum('nf,df->nd', gate_grad, gate_local, preferred_element_type=jnp...]
    convert_element_type x34 -> x0, other arithmetic: 39.6 us -> none  [the longest x32 38.3 us: lap(): part[at].astype(own.dtype)]
    all_gather x2 -> x0, blocking collectives: 29.7 us -> none  [the longest x1 14.9 us: shards(): lax.all_gather(moe_grad, 'head', axis=1, tiled=True)]
  transfers between devices with their start and end apart: 6 -> 0, of which waited for: 2 -> 0; matrix products, arithmetic and copies ran while one was open for 50% -> 0% of each run, Pallas kernels for 0% -> 0%
where the time goes in v1:
time: 97.9 us; the launch traced here: 97.5 us
  Pallas kernels  80.3 us (82%)
  local copies, waits for them, and re-layouts  16.5 us (17%)
    pallas_call x1, Pallas kernels, shards(): pl.pallas_call(functools.partial(kernel, size), out_shape=[jax.ShapeDtype...  80.3 us
    unnamed x24, local copies, waits for them, and re-layouts  16.5 us

profile of v1, /device:TPU:2, one launch (start us, length us, event | category | flops | bytes accessed | tf_op | source)
XLA Modules:
  0.0 97.5 jit_solution(3432775958311722964)
XLA Ops:
  0.6 0.8 copy.19.ids_ref
  1.4 0.8 copy.20.probs_ref
  2.2 6.1 %copy.17.gate_hbm = bf16[1,3072,576]{2,1,0:T(8,128)(2,1)} copy(bf16[1,3072,576]{1,2,0:T(8,128)(2,1)} %param.21) | data formatting | bytes 7077888 | tf_op args[8]
  8.3 0.0 copy-start
  8.3 0.0 copy-start.1
  8.3 0.0 copy-start.2
  8.3 0.0 copy-start.3
  8.3 0.0 copy-start.4
  8.3 0.0 copy-start.5
  8.3 0.0 copy-start.6
  8.4 0.0 copy-start.7
  8.4 6.2 %copy.18.up_hbm = bf16[1,3072,576]{2,1,0:T(8,128)(2,1)} copy(bf16[1,3072,576]{1,2,0:T(8,128)(2,1)} %param.22) | data formatting | bytes 7077888 | tf_op args[9]
  14.5 0.0 copy-done
  14.5 0.0 copy-done.1
  14.5 0.0 copy-done.2
  14.5 0.0 copy-done.3
  14.6 0.0 copy-done.4
  14.6 0.0 copy-done.5
  14.6 0.0 copy-done.6
  14.6 0.0 copy-done.7
  14.6 80.3 %shard_map.156 = (bf16[128,512]{1,0:T(8,128)(2,1)S(1)}, bf16[128,512]{1,0:T(8,128)(2,1)S(1)}, bf16[128,512]{1,0:T(8,128)(2,1)S(1)}, bf16[128,384]{1,0:T(8,128)(2,1)S(1)}) custom-call(bf16[128,512]{1,0:T(8,128)(2,1)S(1)} %copy-done.1, bf16[128,512]{1,0:T(8,128)(2,1)S(1)} %copy-done.2, bf16[128,512]{1,0:T(8,128)(2,1)S(1)} %copy-done.3, ...), custom_call_target="tpu_custom_call" | custom-call | tf_op jit(solution)/shard_map/pallas_call | solution.py:370
  94.9 0.7 copy.25
  95.6 0.7 copy.26
  96.2 0.7 copy.27
  96.9 0.6 copy.28
Async XLA Ops:
  8.3 6.2 %copy-start = (f32[4,128,128]{2,1,0:T(8,128)S(1)}, f32[4,128,128]{2,1,0:T(8,128)}, u32[]{:S(2)}) copy-start(f32[4,128,128]{2,1,0:T(8,128)} %param.18) | copy-start | bytes 786436
  8.3 6.2 %copy-start.1 = (bf16[128,512]{1,0:T(8,128)(2,1)S(1)}, bf16[128,512]{1,0:T(8,128)(2,1)}, u32[]{:S(2)}) copy-start(bf16[128,512]{1,0:T(8,128)(2,1)} %q_ref.1) | copy-start | bytes 393220
  8.3 6.2 %copy-start.2 = (bf16[128,512]{1,0:T(8,128)(2,1)S(1)}, bf16[128,512]{1,0:T(8,128)(2,1)}, u32[]{:S(2)}) copy-start(bf16[128,512]{1,0:T(8,128)(2,1)} %k_ref.1) | copy-start | bytes 393220
  8.3 6.2 %copy-start.3 = (bf16[128,512]{1,0:T(8,128)(2,1)S(1)}, bf16[128,512]{1,0:T(8,128)(2,1)}, u32[]{:S(2)}) copy-start(bf16[128,512]{1,0:T(8,128)(2,1)} %v_ref.1) | copy-start | bytes 393220
  8.3 6.2 %copy-start.4 = (bf16[128,512]{1,0:T(8,128)(2,1)S(1)}, bf16[128,512]{1,0:T(8,128)(2,1)}, u32[]{:S(2)}) copy-start(bf16[128,512]{1,0:T(8,128)(2,1)} %g_ref.1) | copy-start | bytes 393220
  8.3 6.2 %copy-start.5 = (bf16[128,384]{1,0:T(8,128)(2,1)S(1)}, bf16[128,384]{1,0:T(8,128)(2,1)}, u32[]{:S(2)}) copy-start(bf16[128,384]{1,0:T(8,128)(2,1)} %in_ref.1) | copy-start | bytes 294916
  8.3 6.2 %copy-start.6 = (bf16[128,384]{1,0:T(8,128)(2,1)S(1)}, bf16[128,384]{1,0:T(8,128)(2,1)}, u32[]{:S(2)}) copy-start(bf16[128,384]{1,0:T(8,128)(2,1)} %grad_ref.1) | copy-start | bytes 294916
  8.4 6.2 %copy-start.7 = (f32[4,128]{1,0:T(4,128)S(1)}, f32[4,128]{1,0:T(4,128)}, u32[]{:S(2)}) copy-start(f32[4,128]{1,0:T(4,128)} %decay_ref.1) | copy-start | bytes 6148

commit v2 on v1

--- a/solution.py
+++ b/solution.py
@@ -98,20 +98,20 @@
     for load in loads:
         load.start()
 
-    lane = lax.broadcasted_iota(jnp.int32, (T, E), 1)
-    expert = (((y + (lane >> SHIFT)) & (NY - 1)) << SHIFT) + ((z + (lane & (NZ - 1))) & (NZ - 1))
-    first = (ids_ref[:, 0:1] == expert).astype(F32)
-    second = (ids_ref[:, 1:2] == expert).astype(F32)
+    ahead = lax.broadcasted_iota(jnp.int32, (E, T), 0)
+    expert = (((y + (ahead >> SHIFT)) & (NY - 1)) << SHIFT) + ((z + (ahead & (NZ - 1))) & (NZ - 1))
+    first = (ids_ref[0:1, :] == expert).astype(F32)
+    second = (ids_ref[1:2, :] == expert).astype(F32)
     named = first + second
     t_row = lax.broadcasted_iota(jnp.int32, (T, T), 0)
     t_col = lax.broadcasted_iota(jnp.int32, (T, T), 1)
-    earlier = dot((t_row > t_col).astype(F32).astype(BF16), named.astype(BF16))
+    earlier = dot(named.astype(BF16), (t_row < t_col).astype(F32).astype(BF16))
     slot = jnp.where(named > 0.5, earlier, -1.0).astype(BF16)
     r_row = lax.broadcasted_iota(jnp.int32, (E * CAP, E), 0)
     e_col = lax.broadcasted_iota(jnp.int32, (E * CAP, E), 1)
     spread = (r_row // CAP == e_col).astype(F32).astype(BF16)
     want = (lax.broadcasted_iota(jnp.int32, (E * CAP, T), 0) % CAP).astype(F32)
-    pick = (dot_t(spread, slot) == want).astype(F32).astype(BF16)
+    pick = (dot(spread, slot) == want).astype(F32).astype(BF16)
     out_rows[:, 0] = dot(pick, in_ref[...]).astype(BF16).reshape(E, CAP, DC)
     out_rows[:, 1] = dot(pick, grad_ref[...]).astype(BF16).reshape(E, CAP, DC)
 
@@ -168,10 +168,12 @@
         local[1, :, cols] = dot((dot_t(v, g) * within_t).astype(BF16), q)
         local[2, :, cols] = dot((dot_t(k, q) * within_t).astype(BF16), g)
 
-    chance = first * probs_ref[:, 0:1] + second * probs_ref[:, 1:2]
-    pick_t = dot_t(slot, spread) == (lax.broadcasted_iota(jnp.int32, (T, E * CAP), 1) % CAP).astype(F32)
+    chance = first * probs_ref[0:1, :] + second * probs_ref[1:2, :]
+    r_col = lax.broadcasted_iota(jnp.int32, (E, E * CAP), 1)
+    spread_t = (r_col // CAP == lax.broadcasted_iota(jnp.int32, (E, E * CAP), 0)).astype(F32).astype(BF16)
+    pick_t = dot_l(slot, spread_t) == (lax.broadcasted_iota(jnp.int32, (T, E * CAP), 1) % CAP).astype(F32)
     for i, piece in enumerate(pieces(chance, 3)):
-        weights[i] = jnp.where(pick_t, dot_t(piece, spread), 0.0).astype(BF16)
+        weights[i] = jnp.where(pick_t, dot_l(piece, spread_t), 0.0).astype(BF16)
 
     def scan_states():
         own_state.wait()
@@ -248,8 +250,8 @@
             deep = pl.ds(pl.multiple_of(at * W, LANES), W)
             r_in, r_grad = rows[0, at, group(g), :], rows[1, at, group(g), :]
             for acc, value in (
-                (acc_gate, dot(r_in, gate[deep, :])),
-                (acc_up, dot(r_in, up[deep, :])),
+                (acc_gate, dot_t(r_in, gate[:, deep])),
+                (acc_up, dot_t(r_in, up[:, deep])),
                 (acc_hidden, dot_t(r_grad, down[:, deep])),
             ):
                 acc[...] = value if i == 0 else acc[...] + value
@@ -260,7 +262,7 @@
 
         def column(i, carry):
             deep = pl.ds(pl.multiple_of(i * W, LANES), W)
-            part[i, group(g), :] = (dot_t(gate_grad, gate[deep, :]) + dot_t(up_grad, up[deep, :])).astype(BF16)
+            part[i, group(g), :] = (dot(gate_grad, gate[:, deep]) + dot(up_grad, up[:, deep])).astype(BF16)
             return carry
 
         lax.fori_loop(0, NX, column, 0)
@@ -360,6 +362,7 @@
     def shards(queries, keys, values, out_grad, log_decay, prefix_state, moe_input, moe_grad, gate, up, down, ids, probs):
         T, HL = queries.shape[0], log_decay.shape[0]
         DC, D, FL = moe_input.shape[1], gate.shape[1], gate.shape[2]
+        gate, up, ids, probs = (jnp.swapaxes(array, -1, -2) for array in (gate, up, ids, probs))
         CAP = 4 * T // E
         NG = min(4, E // 2)
         ROWS, NR = E * CAP, E * CAP // NG
@@ -373,8 +376,8 @@
             in_specs=[vmem] * 8 + [hbm] * 3 + [vmem] * 2,
             out_specs=[vmem] * 4,
             scratch_shapes=[
-                pltpu.VMEM((D, FL), BF16),
-                pltpu.VMEM((D, FL), BF16),
+                pltpu.VMEM((FL, D), BF16),
+                pltpu.VMEM((FL, D), BF16),
                 pltpu.VMEM((FL, D), BF16),
                 pltpu.VMEM((E, 2, CAP, DC), BF16),
                 pltpu.VMEM((2, NX, ROWS, 2 * DC), BF16),

time: 97.9 us -> 90.7 us (0.926)
  local copies, waits for them, and re-layouts: 16.5 us -> 11 us
  Pallas kernels: 80.3 us -> 78.8 us
    unnamed x24, local copies, waits for them, and re-layouts: 16.5 us -> 11 us
    pallas_call x1, Pallas kernels: 80.3 us -> 78.8 us  [shards(): pl.pallas_call(functools.partial(kernel, size), out_shape=[jax.ShapeDtype...]
where the time goes in v2:
time: 90.7 us; the launch traced here: 90.4 us
  Pallas kernels  78.8 us (87%)
  local copies, waits for them, and re-layouts  11 us (12%)
    pallas_call x1, Pallas kernels, shards(): pl.pallas_call(functools.partial(kernel, size), out_shape=[jax.ShapeDtype...  78.8 us
    unnamed x24, local copies, waits for them, and re-layouts  11 us

profile of v2, /device:TPU:2, one launch (start us, length us, event | category | flops | bytes accessed | tf_op | source)
XLA Modules:
  0.0 90.4 jit_solution(5117175020735943377)
XLA Ops:
  0.6 0.0 copy-start
  0.6 0.9 %copy-done = f32[4,128,128]{2,1,0:T(8,128)S(1)} copy-done((f32[4,128,128]{2,1,0:T(8,128)S(1)}, f32[4,128,128]{2,1,0:T(8,128)}, u32[]{:S(2)}) %copy-start) | copy-done | bytes 262168
  1.6 0.0 copy-start.1
  1.6 0.9 copy-done.1
  2.5 0.0 copy-start.2
  2.5 0.9 copy-done.2
  3.4 0.0 copy-start.3
  3.4 0.9 copy-done.3
  4.3 0.0 copy-start.4
  4.3 0.9 copy-done.4
  5.2 0.0 copy-start.5
  5.2 0.9 copy-done.5
  6.1 0.0 copy-start.6
  6.1 0.9 copy-done.6
  7.0 0.0 copy-start.7
  7.0 0.7 copy-done.7
  7.7 0.0 copy-start.8
  7.7 0.7 copy-done.8
  8.4 0.0 copy-start.9
  8.4 0.7 copy-done.9
  9.0 78.8 %shard_map.156 = (bf16[128,512]{1,0:T(8,128)(2,1)S(1)}, bf16[128,512]{1,0:T(8,128)(2,1)S(1)}, bf16[128,512]{1,0:T(8,128)(2,1)S(1)}, bf16[128,384]{1,0:T(8,128)(2,1)S(1)}) custom-call(bf16[128,512]{1,0:T(8,128)(2,1)S(1)} %copy-done.1, bf16[128,512]{1,0:T(8,128)(2,1)S(1)} %copy-done.2, bf16[128,512]{1,0:T(8,128)(2,1)S(1)} %copy-done.3, ...), custom_call_target="tpu_custom_call" | custom-call | tf_op jit(solution)/shard_map/pallas_call | solution.py:373
  87.8 0.7 copy.21
  88.5 0.7 copy.22
  89.1 0.7 copy.23
  89.8 0.6 copy.24
Async XLA Ops:
  0.6 1.0 %copy-start = (f32[4,128,128]{2,1,0:T(8,128)S(1)}, f32[4,128,128]{2,1,0:T(8,128)}, u32[]{:S(2)}) copy-start(f32[4,128,128]{2,1,0:T(8,128)} %param.18) | copy-start | bytes 786436
  1.6 0.9 copy-start.1
  2.5 0.9 copy-start.2
  3.4 0.9 copy-start.3
  4.3 0.9 copy-start.4
  5.2 0.9 copy-start.5
  6.1 0.9 copy-start.6
  7.0 0.7 copy-start.7
  7.7 0.7 copy-start.8
  8.4 0.7 copy-start.9

commit v3 on v2

--- a/solution.py
+++ b/solution.py
@@ -37,17 +37,19 @@
 
 def kernel(
     size,
-    q_ref, k_ref, v_ref, g_ref, decay_ref, prefix_ref, in_ref, grad_ref, gate_hbm, up_hbm, down_hbm, ids_ref, probs_ref,
+    ids_hbm, in_hbm, grad_hbm, decay_hbm, k_hbm, v_hbm, q_hbm, g_hbm, prefix_hbm, probs_hbm, gate_hbm, up_hbm, down_hbm,
     dq_ref, dk_ref, dv_ref, dx_ref,
+    ids_ref, in_ref, grad_ref, decay_ref, k_ref, v_ref, q_ref, g_ref, prefix_ref, probs_ref,
     gate, up, down, out_rows, rows, acc_gate, acc_up, acc_hidden, part, part_in, total, far_left, far_right, near_left,
     near_right, back, table, weights, state_out, state_all, scan_out, state, local, front_s, tail_s,
-    w_sem, one_sem, a2a_recv, ring_recv, sib_recv, send_sem, part_recv, far_recv, near_recv, back_recv,
+    load_sem, one_sem, a2a_recv, ring_recv, sib_recv, send_sem, part_recv, far_recv, near_recv, back_recv,
 ):
     E, NY, NZ, T, CAP, DC, HL, NG = size
     EG = E // NG
     NR = EG * CAP
     HALF = NR // 2
     W = 2 * DC
+    PR = 2 * NR
     SR = HL * LANES // E
     SHIFT = NZ.bit_length() - 1
 
@@ -91,13 +93,17 @@
     for device in (right, left, sibling):
         pl.semaphore_signal(barrier, inc=1, device_id=device, device_id_type=MESH)
 
-    loads = [
-        pltpu.make_async_copy(hbm.at[0], vmem, w_sem.at[i])
-        for i, (hbm, vmem) in enumerate(((gate_hbm, gate), (up_hbm, up), (down_hbm, down)))
-    ]
+    small = (
+        (ids_hbm, ids_ref), (in_hbm, in_ref), (grad_hbm, grad_ref), (decay_hbm, decay_ref), (k_hbm, k_ref), (v_hbm, v_ref),
+        (q_hbm, q_ref), (g_hbm, g_ref), (prefix_hbm, prefix_ref), (probs_hbm, probs_ref),
+    )
+    large = ((gate_hbm.at[0], gate), (up_hbm.at[0], up), (down_hbm.at[0], down))
+    loads = [pltpu.make_async_copy(src, dst, load_sem.at[i]) for i, (src, dst) in enumerate(small + large)]
     for load in loads:
         load.start()
 
+    for load in loads[:3]:
+        load.wait()
     ahead = lax.broadcasted_iota(jnp.int32, (E, T), 0)
     expert = (((y + (ahead >> SHIFT)) & (NY - 1)) << SHIFT) + ((z + (ahead & (NZ - 1))) & (NZ - 1))
     first = (ids_ref[0:1, :] == expert).astype(F32)
@@ -127,6 +133,8 @@
     own.start()
     lax.fori_loop(1, E, dispatch, 0)
 
+    for load in loads[3:8]:
+        load.wait()
     cum = jnp.zeros((HL, T), F32)
     upto = (t_row <= t_col).astype(F32).astype(BF16)
     for piece in pieces(decay_ref[...], 3):
@@ -156,7 +164,7 @@
     own_state.start()
     lax.fori_loop(1, E, states, 0)
 
-    for i in range(HL):
+    def within_block(i):
         cols = slice(i * LANES, (i + 1) * LANES)
         along = jnp.broadcast_to(cum[i : i + 1, :], (T, T))
         down_t = along.T
@@ -168,27 +176,31 @@
         local[1, :, cols] = dot((dot_t(v, g) * within_t).astype(BF16), q)
         local[2, :, cols] = dot((dot_t(k, q) * within_t).astype(BF16), g)
 
-    chance = first * probs_ref[0:1, :] + second * probs_ref[1:2, :]
-    r_col = lax.broadcasted_iota(jnp.int32, (E, E * CAP), 1)
-    spread_t = (r_col // CAP == lax.broadcasted_iota(jnp.int32, (E, E * CAP), 0)).astype(F32).astype(BF16)
-    pick_t = dot_l(slot, spread_t) == (lax.broadcasted_iota(jnp.int32, (T, E * CAP), 1) % CAP).astype(F32)
-    for i, piece in enumerate(pieces(chance, 3)):
-        weights[i] = jnp.where(pick_t, dot_l(piece, spread_t), 0.0).astype(BF16)
-
-    def scan_states():
+    def weigh(_):
+        loads[9].wait()
+        chance = first * probs_ref[0:1, :] + second * probs_ref[1:2, :]
+        r_col = lax.broadcasted_iota(jnp.int32, (E, E * CAP), 1)
+        spread_t = (r_col // CAP == lax.broadcasted_iota(jnp.int32, (E, E * CAP), 0)).astype(F32).astype(BF16)
+        pick_t = dot_l(slot, spread_t) == (lax.broadcasted_iota(jnp.int32, (T, E * CAP), 1) % CAP).astype(F32)
+        for i, piece in enumerate(pieces(chance, 3)):
+            weights[i] = jnp.where(pick_t, dot_l(piece, spread_t), 0.0).astype(BF16)
+
+    def scan_states(_):
+        loads[8].wait()
         own_state.wait()
         arrived(state_all.at[pl.ds(0, (E - 1) * SR), :], one_sem.at[1])
 
-        def step(reverse, column, i, carried):
-            at = E - 1 - i if reverse else i
-            tile = slices(state_all, at)[...].astype(F32)
-            factor = tile[0:1, 2 * LANES :] + tile[1:2, 2 * LANES :] + tile[2:3, 2 * LANES :]
-            columns = slice(column * LANES, (column + 1) * LANES)
-            slices(scan_out, at)[:, columns] = carried.astype(BF16)
-            return factor * carried + tile[:, columns]
-
-        lax.fori_loop(0, E, functools.partial(step, False, 0), slices(prefix_ref, c)[...])
-        lax.fori_loop(0, E, functools.partial(step, True, 1), jnp.zeros((SR, LANES), F32))
+        def step(i, carried):
+            new = []
+            for column, (at, value) in enumerate(zip((i, E - 1 - i), carried)):
+                tile = slices(state_all, at)[...].astype(F32)
+                factor = tile[0:1, 2 * LANES :] + tile[1:2, 2 * LANES :] + tile[2:3, 2 * LANES :]
+                columns = slice(column * LANES, (column + 1) * LANES)
+                slices(scan_out, at)[:, columns] = value.astype(BF16)
+                new.append(factor * value + tile[:, columns])
+            return tuple(new)
+
+        lax.fori_loop(0, E, step, (slices(prefix_ref, c)[...], jnp.zeros((SR, LANES), F32)), unroll=4)
 
         def give(d, carry):
             remote(slices(scan_out, forth(d)), slices(state, c), send_sem.at[2], one_sem.at[3], (forth(d), h)).start()
@@ -199,16 +211,16 @@
 
     own_scan = pltpu.make_async_copy(slices(scan_out, c), slices(state, c), one_sem.at[4])
 
-    def finish_states():
-        own_scan.wait()
-        arrived(state.at[pl.ds(0, (E - 1) * SR), :], one_sem.at[3])
-        for i in range(HL):
-            cols = slice(i * LANES, (i + 1) * LANES)
-            k, v, g = k_ref[:, cols], v_ref[:, cols], g_ref[:, cols]
-            s_in, s_grad = state[cols, 0:LANES], state[cols, LANES : 2 * LANES]
-            dq_ref[:, cols] = (local[0, :, cols] + front_s[i] * dot_t(g, s_in)).astype(BF16)
-            dk_ref[:, cols] = (local[1, :, cols] + tail_s[i] * dot_t(v, s_grad)).astype(BF16)
-            dv_ref[:, cols] = (local[2, :, cols] + tail_s[i] * dot(k, s_grad)).astype(BF16)
+    def finish_states(i):
+        if i == 0:
+            own_scan.wait()
+            arrived(state.at[pl.ds(0, (E - 1) * SR), :], one_sem.at[3])
+        cols = slice(i * LANES, (i + 1) * LANES)
+        k, v, g = k_ref[:, cols], v_ref[:, cols], g_ref[:, cols]
+        s_in, s_grad = state[cols, 0:LANES], state[cols, LANES : 2 * LANES]
+        dq_ref[:, cols] = (local[0, :, cols] + front_s[i] * dot_t(g, s_in)).astype(BF16)
+        dk_ref[:, cols] = (local[1, :, cols] + tail_s[i] * dot_t(v, s_grad)).astype(BF16)
+        dv_ref[:, cols] = (local[2, :, cols] + tail_s[i] * dot(k, s_grad)).astype(BF16)
 
     def to_sibling(ref, which, send):
         remote(ref, ref, send_sem.at[send], sib_recv.at[which], sibling).start()
@@ -240,43 +252,45 @@
             arrived(ref, ring_recv.at[g, 2 + i])
             to_sibling(ref, (g, 3 + i), 10 + i)
 
-    def expert(g):
-        for i, at in enumerate((x, x_left, x_right, x_far)):
+    def expert_in(p, i):
+        at = (x, x_left, x_right, x_far)[i]
+        for g in (2 * p, 2 * p + 1):
             if i < 3:
                 arrived(rows.at[:, at, group(g), other], sib_recv.at[g, i])
             else:
                 arrived(rows.at[0, at, group(g), other], sib_recv.at[g, 3])
                 arrived(rows.at[1, at, group(g), other], sib_recv.at[g, 4])
-            deep = pl.ds(pl.multiple_of(at * W, LANES), W)
-            r_in, r_grad = rows[0, at, group(g), :], rows[1, at, group(g), :]
-            for acc, value in (
-                (acc_gate, dot_t(r_in, gate[:, deep])),
-                (acc_up, dot_t(r_in, up[:, deep])),
-                (acc_hidden, dot_t(r_grad, down[:, deep])),
-            ):
-                acc[...] = value if i == 0 else acc[...] + value
-        gate_pre, up_pre, hidden = acc_gate[...], acc_up[...], acc_hidden[...]
+        if p == 0 and i == 0:
+            for load in loads[10:]:
+                load.wait()
+        deep = pl.ds(pl.multiple_of(at * W, LANES), W)
+        r_in, r_grad = rows[0, at, pl.ds(p * PR, PR), :], rows[1, at, pl.ds(p * PR, PR), :]
+        for acc, r, weight in ((acc_gate, r_in, gate), (acc_up, r_in, up), (acc_hidden, r_grad, down)):
+            value = dot_t(r, weight[:, deep])
+            acc[p] = value if i == 0 else acc[p] + value
+
+    def expert_out(p):
+        gate_pre, up_pre, hidden = acc_gate[p], acc_up[p], acc_hidden[p]
         sig = 1.0 / (1.0 + jnp.exp(-gate_pre))
         gate_grad = (hidden * up_pre * sig * (1.0 + gate_pre * (1.0 - sig))).astype(BF16)
         up_grad = (hidden * gate_pre * sig).astype(BF16)
-
-        def column(i, carry):
-            deep = pl.ds(pl.multiple_of(i * W, LANES), W)
-            part[i, group(g), :] = (dot(gate_grad, gate[:, deep]) + dot(up_grad, up[:, deep])).astype(BF16)
-            return carry
-
-        lax.fori_loop(0, NX, column, 0)
-
-    def reduce_1(g):
-        remote(
-            part.at[:, group(g), other], part_in.at[:, group(g), :], send_sem.at[12], part_recv.at[g], sibling
-        ).start()
+        span = pl.ds(p * PR, PR)
+        for i, at in enumerate((x_far, x_right, x_left, x)):
+            deep = pl.ds(pl.multiple_of(at * W, LANES), W)
+            part[at, span, :] = (dot(gate_grad, gate[:, deep]) + dot(up_grad, up[:, deep])).astype(BF16)
+            remote(
+                part.at[at, span, other], part_in.at[at, span, :], send_sem.at[12], part_recv.at[p, i], sibling
+            ).start()
+
+    def from_sibling(g, i, at):
+        if g % 2 == 0:
+            arrived(part_in.at[at, pl.ds(g * NR, PR), :], part_recv.at[g // 2, i])
 
     def pair_sum(at, span):
         return part[at, span, mine].astype(F32) + part_in[at, span, :].astype(F32)
 
     def reduce_2(g):
-        arrived(part_in.at[:, group(g), :], part_recv.at[g])
+        from_sibling(g, 0, x_far)
         total[0, group(g), :] = pair_sum(x_far, group(g)).astype(BF16)
         remote(
             total.at[0, pl.ds(g * NR, HALF), :], far_left.at[pl.ds(g * HALF, HALF), :], send_sem.at[13], far_recv.at[g, 0], right
@@ -288,12 +302,14 @@
     def reduce_3(g):
         half = pl.ds(g * HALF, HALF)
         lower, upper = pl.ds(g * NR, HALF), pl.ds(g * NR + HALF, HALF)
+        from_sibling(g, 1, x_right)
         arrived(far_left.at[half, :], far_recv.at[g, 0])
         total[1, lower, :] = (pair_sum(x_right, lower) + far_left[half, :].astype(F32)).astype(BF16)
         total[1, upper, :] = pair_sum(x_right, upper).astype(BF16)
         remote(
             total.at[1, group(g), :], near_left.at[group(g), :], send_sem.at[15], near_recv.at[g, 0], right
         ).start()
+        from_sibling(g, 2, x_left)
         arrived(far_right.at[half, :], far_recv.at[g, 1])
         total[2, lower, :] = pair_sum(x_left, lower).astype(BF16)
         total[2, upper, :] = (pair_sum(x_left, upper) + far_right[half, :].astype(F32)).astype(BF16)
@@ -307,6 +323,7 @@
     own_back = pltpu.make_async_copy(slots(back, 0), slots(table, 0), one_sem.at[5])
 
     def reduce_4(g):
+        from_sibling(g, 3, x)
         arrived(near_left.at[group(g), :], near_recv.at[g, 0])
         arrived(near_right.at[group(g), :], near_recv.at[g, 1])
         value = near_left[group(g), :].astype(F32) + near_right[group(g), :].astype(F32)
@@ -320,22 +337,24 @@
             own_back.start()
         lax.fori_loop(max(g * EG, 1), (g + 1) * EG, give, 0)
 
-    for load in loads:
-        load.wait()
-    for i in range(NG + 5):
-        for ahead, stage in enumerate((gather_1, gather_2, gather_3)):
-            if 0 <= i - ahead < NG:
-                stage(i - ahead)
-        if i == NG - 1:
-            scan_states()
-        if 0 <= i - 2 < NG:
-            expert(i - 2)
-            reduce_1(i - 2)
-        if i == NG + 1:
-            finish_states()
-        for ahead, stage in ((3, reduce_2), (4, reduce_3), (5, reduce_4)):
-            if 0 <= i - ahead < NG:
-                stage(i - ahead)
+    last = 20.5 + 9.6 * (NG // 2 - 1)
+    plan = [(last - 6.6, scan_states, 0), (16.5, weigh, 0)]
+    for g in range(NG):
+        plan += [(4 + 4 * g, gather_1, g), (9 + 5.2 * g, gather_2, g), (14.6 + 4.8 * g, gather_3, g)]
+    for i, at in enumerate((5, 6, 13, 13.1)[:HL]):
+        plan.append((at, within_block, i))
+    for p in range(NG // 2):
+        for i, at in enumerate((9.5 + 8 * p, 15.4 + 10.4 * p, 15.5 + 10.4 * p, 20.4 + 9.6 * p)):
+            plan.append((at, functools.partial(expert_in, p), i))
+        out = 20.5 + 9.6 * p
+        plan.append((out, expert_out, p))
+        for g in (0, 1):
+            for stage, at in ((reduce_2, 2 + g * 0.1), (reduce_3, 4.5 + g * 0.1), (reduce_4, 8 + g)):
+                plan.append((out + at, stage, 2 * p + g))
+    for i in range(HL):
+        plan.append((last + (2.5, 2.6, 5, 5.1)[i], finish_states, i))
+    for _, stage, which in sorted(plan, key=lambda entry: entry[0]):
+        stage(which)
 
     own_back.wait()
     arrived(table.at[pl.ds(0, (E - 1) * CAP), :], back_recv.at[0])
@@ -355,6 +374,14 @@
         sent(ref, send_sem.at[i])
 
 
+def copy_out(*refs):
+    copies = [pltpu.make_async_copy(refs[i], refs[4 + i], refs[8].at[i]) for i in range(4)]
+    for copy in copies:
+        copy.start()
+    for copy in copies:
+        copy.wait()
+
+
 def solution(mesh):
     E = mesh.shape["ctx"]
     NZ = min(8, E // 2)
@@ -367,23 +394,29 @@
         NG = min(4, E // 2)
         ROWS, NR = E * CAP, E * CAP // NG
         vmem = pl.BlockSpec(memory_space=pltpu.VMEM)
-        hbm = pl.BlockSpec(memory_space=pl.ANY)
+        hbm = pl.BlockSpec(memory_space=pltpu.HBM)
         size = (E, E // NZ, NZ, T, CAP, DC, HL, NG)
         dma = pltpu.SemaphoreType.DMA
-        return pl.pallas_call(
+        results = [jax.ShapeDtypeStruct((T, HL * LANES), BF16)] * 3 + [jax.ShapeDtypeStruct((T, DC), BF16)]
+        small = (
+            ids, moe_input, moe_grad, log_decay, keys, values, queries, out_grad,
+            prefix_state.reshape(HL * LANES, LANES), probs,
+        )
+        made = pl.pallas_call(
             functools.partial(kernel, size),
-            out_shape=[jax.ShapeDtypeStruct((T, HL * LANES), BF16)] * 3 + [jax.ShapeDtypeStruct((T, DC), BF16)],
-            in_specs=[vmem] * 8 + [hbm] * 3 + [vmem] * 2,
+            out_shape=results,
+            in_specs=[hbm] * 13,
             out_specs=[vmem] * 4,
-            scratch_shapes=[
+            scratch_shapes=[pltpu.VMEM(array.shape, array.dtype) for array in small]
+            + [
                 pltpu.VMEM((FL, D), BF16),
                 pltpu.VMEM((FL, D), BF16),
                 pltpu.VMEM((FL, D), BF16),
                 pltpu.VMEM((E, 2, CAP, DC), BF16),
                 pltpu.VMEM((2, NX, ROWS, 2 * DC), BF16),
-                pltpu.VMEM((NR, FL), F32),
-                pltpu.VMEM((NR, FL), F32),
-                pltpu.VMEM((NR, FL), F32),
+                pltpu.VMEM((NG // 2, 2 * NR, FL), F32),
+                pltpu.VMEM((NG // 2, 2 * NR, FL), F32),
+                pltpu.VMEM((NG // 2, 2 * NR, FL), F32),
                 pltpu.VMEM((NX, ROWS, 2 * DC), BF16),
                 pltpu.VMEM((NX, ROWS, DC), BF16),
                 pltpu.VMEM((3, ROWS, DC), BF16),
@@ -401,13 +434,13 @@
                 pltpu.VMEM((3, T, HL * LANES), F32),
                 pltpu.VMEM((HL, T, LANES), F32),
                 pltpu.VMEM((HL, T, LANES), F32),
-                dma((3,)),
+                dma((13,)),
                 dma((6,)),
                 dma((NG,)),
                 dma((NG, 4)),
                 dma((NG, 5)),
                 dma((18,)),
-                dma((NG,)),
+                dma((NG // 2, 4)),
                 dma((NG, 2)),
                 dma((NG, 2)),
                 dma((1,)),
@@ -415,10 +448,14 @@
             compiler_params=pltpu.CompilerParams(
                 collective_id=0, has_side_effects=True, vmem_limit_bytes=52 * 1024 * 1024
             ),
-        )(
-            queries, keys, values, out_grad, log_decay, prefix_state.reshape(HL * LANES, LANES),
-            moe_input, moe_grad, gate, up, down, ids, probs,
-        )
+        )(*(pltpu.with_memory_space_constraint(array, pltpu.HBM) for array in (*small, gate, up, down)))
+        return pl.pallas_call(
+            copy_out,
+            out_shape=results,
+            in_specs=[vmem] * 4,
+            out_specs=[hbm] * 4,
+            scratch_shapes=[dma((4,))],
+        )(*(pltpu.with_memory_space_constraint(array, pltpu.VMEM) for array in made))
 
     in_specs = (
         P("ctx", "head"),

time: 90.7 us -> 79.1 us (0.87)
  local copies, waits for them, and re-layouts: 11 us -> 0 us
  Pallas kernels: 78.8 us -> 77.7 us
    unnamed x24 -> x0, local copies, waits for them, and re-layouts: 11 us -> none
    pallas_call x1 -> x2, Pallas kernels: 78.8 us -> 77.7 us  [the longest x1 76.9 us: shards(): pl.pallas_call(functools.partial(kernel, size), out_shape=results, in_spe...]
where the time goes in v3:
time: 79.1 us; the launch traced here: 78.5 us
  Pallas kernels  77.7 us (98%)
  between operations  0.81 us (1%)
    pallas_call x1, Pallas kernels, shards(): pl.pallas_call(functools.partial(kernel, size), out_shape=results, in_spe...  76.9 us

profile of v3, /device:TPU:2, one launch (start us, length us, event | category | flops | bytes accessed | tf_op | source)
XLA Modules:
  0.0 78.5 jit_solution(9253485609750322805)
XLA Ops:
  0.6 76.9 %shard_map.156 = (bf16[128,512]{1,0:T(8,128)(2,1)S(1)}, bf16[128,512]{1,0:T(8,128)(2,1)S(1)}, bf16[128,512]{1,0:T(8,128)(2,1)S(1)}, bf16[128,384]{1,0:T(8,128)(2,1)S(1)}) custom-call(s32[2,128]{1,0:T(2,128)} %bitcast.8, bf16[128,384]{1,0:T(8,128)(2,1)} %in_hbm.1, bf16[128,384]{1,0:T(8,128)(2,1)} %grad_hbm.1, f32[4,128]{1,0:T(4,128)} %decay_hbm.1, ...), custom_call_target="tpu_custom_call" | custom-call | tf_op jit(solution)/shard_map/pallas_call | solution.py:405
  77.5 0.8 %shard_map.157 = (bf16[128,512]{1,0:T(8,128)(2,1)}, bf16[128,512]{1,0:T(8,128)(2,1)}, bf16[128,512]{1,0:T(8,128)(2,1)}, bf16[128,384]{1,0:T(8,128)(2,1)}) custom-call(bf16[128,512]{1,0:T(8,128)(2,1)S(1)} %get-tuple-element.8.refs_0_, bf16[128,512]{1,0:T(8,128)(2,1)S(1)} %get-tuple-element.9.refs_1_, bf16[128,512]{1,0:T(8,128)(2,1)S(1)} %get-tuple-element.10.refs_2_, ...), custom_call_target="tpu_custom_call" | custom-call | tf_op jit(solution)/shard_map/pallas_call | solution.py:452

commit v4 on v3

--- a/solution.py
+++ b/solution.py
@@ -35,12 +35,65 @@
     return parts
 
 
+RANK = dict(s1=0, s2=0, s3=0, r2=1, near=1, r3=1, r4=1, mix=4, mid=2, out=2, scan=2.5, finish=3.5, within=4, weigh=4)
+RANK["in"] = 2
+
+
+def order(groups, rank):
+    pairs, q = groups // 2, 4.0 / groups
+    stages = {}
+
+    def add(name, cost, needs, sends=()):
+        stages[name] = (cost, needs, sends)
+
+    came = {("disp", g): 1.0 + 5.6 * q * (g + 1) for g in range(groups)}
+    came["states"] = 1.0 + 5.6 * q * groups + 4
+    free = {"x": 0.0, "sib": 0.0, "z": came["states"]}
+    for g in range(groups):
+        p = g // 2
+        add(("s1", g), 0.2, [("disp", g)], [(("l1", g), "x", 4.4 * q), (("b", 0, g), "sib", 0.8 * q)])
+        add(("s2", g), 0.3, [("l1", g)], [(("l2", g), "x", 2.2 * q), (("b", 1, g), "sib", 0.8 * q), (("b", 2, g), "sib", 0.8 * q)])
+        add(("s3", g), 0.3, [("l2", g)], [(("b", 3, g), "sib", 0.8 * q)])
+        add(("r2", g), 0.4, [("c", p, 0)], [(("f", g), "x", 1.1 * q)])
+        add(("near", g), 0.3, [("c", p, 1), ("c", p, 2)], [(("m", g), "x", 1.1 * q)])
+        add(("r3", g), 0.4, [("f", g), ("c", p, 1), ("c", p, 2)], [(("n", g), "x", 1.1 * q)])
+        add(("r4", g), 0.7, [("m", g), ("n", g), ("c", p, 3)], [(("t", g), "z", 2.2 * q)])
+    for p in range(pairs):
+        for i in range(4):
+            add(("in", p, i), 1.05 * q, [("b", i, 2 * p), ("b", i, 2 * p + 1)] + [("in", p, j) for j in range(i)])
+            add(("out", p, i), 0.7 * q, [("mid", p)] + [("out", p, j) for j in range(i)], [(("c", p, i), "sib", 0.5)])
+        add(("mix", p), 0.5, [("t", 2 * p), ("t", 2 * p + 1), ("weigh",)])
+        add(("mid", p), 0.4 * q, [("in", p, i) for i in range(4)])
+    for i in range(4):
+        add(("within", i), 0.9, [])
+        add(("finish", i), 0.5, ["scanned", ("within", i)])
+    add(("weigh",), 1.0, [])
+    add(("scan",), 2.0, ["states"], [("scanned", "z", 5.5)])
+    done, now = [], 3.0
+    while len(done) < len(stages):
+        ready = []
+        for name, (cost, needs, sends) in stages.items():
+            if name not in done and all(n in came for n in needs):
+                ready.append((max([0.0] + [came[n] for n in needs]), name))
+        start = min(at for at, _ in ready)
+        now = max(now, start)
+        _, name = min((rank[name[0]] + 0.01 * sum(name[1:2]), name) for at, name in ready if at <= now)
+        cost, needs, sends = stages[name]
+        now += cost
+        done.append(name)
+        came[name] = now
+        for event, link, took in sends:
+            free[link] = max(free[link], now) + took
+            came[event] = free[link] + 1.6
+    return done
+
+
 def kernel(
     size,
     ids_hbm, in_hbm, grad_hbm, decay_hbm, k_hbm, v_hbm, q_hbm, g_hbm, prefix_hbm, probs_hbm, gate_hbm, up_hbm, down_hbm,
     dq_ref, dk_ref, dv_ref, dx_ref,
     ids_ref, in_ref, grad_ref, decay_ref, k_ref, v_ref, q_ref, g_ref, prefix_ref, probs_ref,
-    gate, up, down, out_rows, rows, acc_gate, acc_up, acc_hidden, part, part_in, total, far_left, far_right, near_left,
+    gate, up, down, out_rows, rows, acc_gate, acc_up, acc_hidden, gate_s, up_s, mixed, part, part_in, total, far_left, far_right, near_left,
     near_right, back, table, weights, state_out, state_all, scan_out, state, local, front_s, tail_s,
     load_sem, one_sem, a2a_recv, ring_recv, sib_recv, send_sem, part_recv, far_recv, near_recv, back_recv,
 ):
@@ -164,6 +217,8 @@
     own_state.start()
     lax.fori_loop(1, E, states, 0)
 
+    seen = set()
+
     def within_block(i):
         cols = slice(i * LANES, (i + 1) * LANES)
         along = jnp.broadcast_to(cum[i : i + 1, :], (T, T))
@@ -176,7 +231,7 @@
         local[1, :, cols] = dot((dot_t(v, g) * within_t).astype(BF16), q)
         local[2, :, cols] = dot((dot_t(k, q) * within_t).astype(BF16), g)
 
-    def weigh(_):
+    def weigh():
         loads[9].wait()
         chance = first * probs_ref[0:1, :] + second * probs_ref[1:2, :]
         r_col = lax.broadcasted_iota(jnp.int32, (E, E * CAP), 1)
@@ -185,7 +240,7 @@
         for i, piece in enumerate(pieces(chance, 3)):
             weights[i] = jnp.where(pick_t, dot_l(piece, spread_t), 0.0).astype(BF16)
 
-    def scan_states(_):
+    def scan_states():
         loads[8].wait()
         own_state.wait()
         arrived(state_all.at[pl.ds(0, (E - 1) * SR), :], one_sem.at[1])
@@ -212,7 +267,8 @@
     own_scan = pltpu.make_async_copy(slices(scan_out, c), slices(state, c), one_sem.at[4])
 
     def finish_states(i):
-        if i == 0:
+        if "state" not in seen:
+            seen.add("state")
             own_scan.wait()
             arrived(state.at[pl.ds(0, (E - 1) * SR), :], one_sem.at[3])
         cols = slice(i * LANES, (i + 1) * LANES)
@@ -260,7 +316,8 @@
             else:
                 arrived(rows.at[0, at, group(g), other], sib_recv.at[g, 3])
                 arrived(rows.at[1, at, group(g), other], sib_recv.at[g, 4])
-        if p == 0 and i == 0:
+        if "weights" not in seen:
+            seen.add("weights")
             for load in loads[10:]:
                 load.wait()
         deep = pl.ds(pl.multiple_of(at * W, LANES), W)
@@ -269,21 +326,24 @@
             value = dot_t(r, weight[:, deep])
             acc[p] = value if i == 0 else acc[p] + value
 
-    def expert_out(p):
+    def expert_mid(p):
         gate_pre, up_pre, hidden = acc_gate[p], acc_up[p], acc_hidden[p]
         sig = 1.0 / (1.0 + jnp.exp(-gate_pre))
-        gate_grad = (hidden * up_pre * sig * (1.0 + gate_pre * (1.0 - sig))).astype(BF16)
-        up_grad = (hidden * gate_pre * sig).astype(BF16)
+        gate_s[p] = (hidden * up_pre * sig * (1.0 + gate_pre * (1.0 - sig))).astype(BF16)
+        up_s[p] = (hidden * gate_pre * sig).astype(BF16)
+
+    def expert_out(p, i):
+        at = (x_far, x_right, x_left, x)[i]
         span = pl.ds(p * PR, PR)
-        for i, at in enumerate((x_far, x_right, x_left, x)):
-            deep = pl.ds(pl.multiple_of(at * W, LANES), W)
-            part[at, span, :] = (dot(gate_grad, gate[:, deep]) + dot(up_grad, up[:, deep])).astype(BF16)
-            remote(
-                part.at[at, span, other], part_in.at[at, span, :], send_sem.at[12], part_recv.at[p, i], sibling
-            ).start()
+        deep = pl.ds(pl.multiple_of(at * W, LANES), W)
+        part[at, span, :] = (dot(gate_s[p], gate[:, deep]) + dot(up_s[p], up[:, deep])).astype(BF16)
+        remote(
+            part.at[at, span, other], part_in.at[at, span, :], send_sem.at[12], part_recv.at[p, i], sibling
+        ).start()
 
     def from_sibling(g, i, at):
-        if g % 2 == 0:
+        if (g // 2, i) not in seen:
+            seen.add((g // 2, i))
             arrived(part_in.at[at, pl.ds(g * NR, PR), :], part_recv.at[g // 2, i])
 
     def pair_sum(at, span):
@@ -299,23 +359,35 @@
             total.at[0, pl.ds(g * NR + HALF, HALF), :], far_right.at[pl.ds(g * HALF, HALF), :], send_sem.at[14], far_recv.at[g, 1], left
         ).start()
 
+    def halves(g):
+        return pl.ds(g * NR, HALF), pl.ds(g * NR + HALF, HALF)
+
+    def to_right(span, recv):
+        remote(total.at[1, span, :], near_left.at[span, :], send_sem.at[15], recv, right).start()
+
+    def to_left(span, recv):
+        remote(total.at[2, span, :], near_right.at[span, :], send_sem.at[16], recv, left).start()
+
+    def reduce_near(g):
+        lower, upper = halves(g)
+        from_sibling(g, 1, x_right)
+        total[1, upper, :] = pair_sum(x_right, upper).astype(BF16)
+        to_right(upper, near_recv.at[g, 0])
+        from_sibling(g, 2, x_left)
+        total[2, lower, :] = pair_sum(x_left, lower).astype(BF16)
+        to_left(lower, near_recv.at[g, 1])
+
     def reduce_3(g):
         half = pl.ds(g * HALF, HALF)
-        lower, upper = pl.ds(g * NR, HALF), pl.ds(g * NR + HALF, HALF)
+        lower, upper = halves(g)
         from_sibling(g, 1, x_right)
         arrived(far_left.at[half, :], far_recv.at[g, 0])
         total[1, lower, :] = (pair_sum(x_right, lower) + far_left[half, :].astype(F32)).astype(BF16)
-        total[1, upper, :] = pair_sum(x_right, upper).astype(BF16)
-        remote(
-            total.at[1, group(g), :], near_left.at[group(g), :], send_sem.at[15], near_recv.at[g, 0], right
-        ).start()
+        to_right(lower, near_recv.at[g, 2])
         from_sibling(g, 2, x_left)
         arrived(far_right.at[half, :], far_recv.at[g, 1])
-        total[2, lower, :] = pair_sum(x_left, lower).astype(BF16)
         total[2, upper, :] = (pair_sum(x_left, upper) + far_right[half, :].astype(F32)).astype(BF16)
-        remote(
-            total.at[2, group(g), :], near_right.at[group(g), :], send_sem.at[16], near_recv.at[g, 1], left
-        ).start()
+        to_left(upper, near_recv.at[g, 3])
 
     def slots(ref, d):
         return ref.at[pl.ds(pl.multiple_of(d * CAP, CAP), CAP), :]
@@ -324,42 +396,43 @@
 
     def reduce_4(g):
         from_sibling(g, 3, x)
-        arrived(near_left.at[group(g), :], near_recv.at[g, 0])
-        arrived(near_right.at[group(g), :], near_recv.at[g, 1])
+        lower, upper = halves(g)
+        arrived(near_left.at[upper, :], near_recv.at[g, 0])
+        arrived(near_right.at[lower, :], near_recv.at[g, 1])
+        arrived(near_left.at[lower, :], near_recv.at[g, 2])
+        arrived(near_right.at[upper, :], near_recv.at[g, 3])
         value = near_left[group(g), :].astype(F32) + near_right[group(g), :].astype(F32)
         back[group(g), :] = (pair_sum(x, group(g)) + value).astype(BF16)
 
         def give(d, carry):
-            remote(slots(back, d), slots(table, d), send_sem.at[17], back_recv.at[0], (back_to(d), h)).start()
+            remote(slots(back, d), slots(table, d), send_sem.at[17], back_recv.at[g // 2], (back_to(d), h)).start()
             return carry
 
         if g == 0:
             own_back.start()
         lax.fori_loop(max(g * EG, 1), (g + 1) * EG, give, 0)
 
-    last = 20.5 + 9.6 * (NG // 2 - 1)
-    plan = [(last - 6.6, scan_states, 0), (16.5, weigh, 0)]
-    for g in range(NG):
-        plan += [(4 + 4 * g, gather_1, g), (9 + 5.2 * g, gather_2, g), (14.6 + 4.8 * g, gather_3, g)]
-    for i, at in enumerate((5, 6, 13, 13.1)[:HL]):
-        plan.append((at, within_block, i))
-    for p in range(NG // 2):
-        for i, at in enumerate((9.5 + 8 * p, 15.4 + 10.4 * p, 15.5 + 10.4 * p, 20.4 + 9.6 * p)):
-            plan.append((at, functools.partial(expert_in, p), i))
-        out = 20.5 + 9.6 * p
-        plan.append((out, expert_out, p))
-        for g in (0, 1):
-            for stage, at in ((reduce_2, 2 + g * 0.1), (reduce_3, 4.5 + g * 0.1), (reduce_4, 8 + g)):
-                plan.append((out + at, stage, 2 * p + g))
-    for i in range(HL):
-        plan.append((last + (2.5, 2.6, 5, 5.1)[i], finish_states, i))
-    for _, stage, which in sorted(plan, key=lambda entry: entry[0]):
-        stage(which)
-
-    own_back.wait()
-    arrived(table.at[pl.ds(0, (E - 1) * CAP), :], back_recv.at[0])
-    found = table[...]
-    dx_ref[...] = (dot(weights[0], found) + dot(weights[1], found) + dot(weights[2], found)).astype(BF16)
+    def mix(p):
+        lead = CAP if p == 0 else 0
+        if p == 0:
+            own_back.wait()
+        arrived(table.at[pl.ds(p * PR + lead, PR - lead), :], back_recv.at[p])
+        found, span = table[pl.ds(p * PR, PR), :], pl.ds(p * PR, PR)
+        value = dot(weights[0, :, span], found) + dot(weights[1, :, span], found) + dot(weights[2, :, span], found)
+        if p > 0:
+            value = value + mixed[...]
+        if p < NG // 2 - 1:
+            mixed[...] = value
+        else:
+            dx_ref[...] = value.astype(BF16)
+
+    run = dict(
+        s1=gather_1, s2=gather_2, s3=gather_3, mid=expert_mid, near=reduce_near, mix=mix, out=expert_out, r2=reduce_2, r3=reduce_3, r4=reduce_4,
+        within=within_block, weigh=weigh, scan=scan_states, finish=finish_states,
+    )
+    run["in"] = expert_in
+    for name in order(NG, RANK):
+        run[name[0]](*name[1:])
 
     ring, half_ring = rows.at[:, 0, :, 0:DC], rows.at[0, 0, :, 0:DC]
     for i, ref in (
@@ -417,6 +490,9 @@
                 pltpu.VMEM((NG // 2, 2 * NR, FL), F32),
                 pltpu.VMEM((NG // 2, 2 * NR, FL), F32),
                 pltpu.VMEM((NG // 2, 2 * NR, FL), F32),
+                pltpu.VMEM((NG // 2, 2 * NR, FL), BF16),
+                pltpu.VMEM((NG // 2, 2 * NR, FL), BF16),
+                pltpu.VMEM((T, DC), F32),
                 pltpu.VMEM((NX, ROWS, 2 * DC), BF16),
                 pltpu.VMEM((NX, ROWS, DC), BF16),
                 pltpu.VMEM((3, ROWS, DC), BF16),
@@ -442,8 +518,8 @@
                 dma((18,)),
                 dma((NG // 2, 4)),
                 dma((NG, 2)),
-                dma((NG, 2)),
-                dma((1,)),
+                dma((NG, 4)),
+                dma((NG // 2,)),
             ],
             compiler_params=pltpu.CompilerParams(
                 collective_id=0, has_side_effects=True, vmem_limit_bytes=52 * 1024 * 1024

time: 79.1 us -> 74.2 us (0.938)
  Pallas kernels: 77.7 us -> 72.9 us
    pallas_call x1, Pallas kernels: 76.9 us -> 72 us  [shards(): pl.pallas_call(functools.partial(kernel, size), out_shape=results, in_spe...]
where the time goes in v4:
time: 74.2 us; the launch traced here: 73.7 us
  Pallas kernels  72.9 us (98%)
  between operations  0.81 us (1%)
    pallas_call x1, Pallas kernels, shards(): pl.pallas_call(functools.partial(kernel, size), out_shape=results, in_spe...  72 us

profile of v4, /device:TPU:2, one launch (start us, length us, event | category | flops | bytes accessed | tf_op | source)
XLA Modules:
  0.0 73.7 jit_solution(17294813233777053270)
XLA Ops:
  0.6 72.0 %shard_map.156 = (bf16[128,512]{1,0:T(8,128)(2,1)S(1)}, bf16[128,512]{1,0:T(8,128)(2,1)S(1)}, bf16[128,512]{1,0:T(8,128)(2,1)S(1)}, bf16[128,384]{1,0:T(8,128)(2,1)S(1)}) custom-call(s32[2,128]{1,0:T(2,128)} %bitcast.8, bf16[128,384]{1,0:T(8,128)(2,1)} %in_hbm.1, bf16[128,384]{1,0:T(8,128)(2,1)} %grad_hbm.1, f32[4,128]{1,0:T(4,128)} %decay_hbm.1, ...), custom_call_target="tpu_custom_call" | custom-call | tf_op jit(solution)/shard_map/pallas_call | solution.py:478
  72.7 0.8 %shard_map.157 = (bf16[128,512]{1,0:T(8,128)(2,1)}, bf16[128,512]{1,0:T(8,128)(2,1)}, bf16[128,512]{1,0:T(8,128)(2,1)}, bf16[128,384]{1,0:T(8,128)(2,1)}) custom-call(bf16[128,512]{1,0:T(8,128)(2,1)S(1)} %get-tuple-element.8.refs_0_, bf16[128,512]{1,0:T(8,128)(2,1)S(1)} %get-tuple-element.9.refs_1_, bf16[128,512]{1,0:T(8,128)(2,1)S(1)} %get-tuple-element.10.refs_2_, ...), custom_call_target="tpu_custom_call" | custom-call | tf_op jit(solution)/shard_map/pallas_call | solution.py:528
